TPU v7x, 256 devices: a whole 4x4x8 slice. The times are simulated.
256 devices in a mesh: band: 64 (over y, z, core), lev: 4 (over x).
Axes of the slice: x: 4, y: 4, z: 8, core: 2. Of those that a mesh axis runs over, the one named last changes fastest.
Arguments:
- spectral: float32 [5376, 16, 128], P('band', 'lev'), may hold values from -6 to 6
- legendre: bfloat16 [5376, 64, 1024], P('band'), may hold values from -0.15625 to 0.15625
- wave_ids: int32 [512], P('band'), may hold values from 0 to 1279, as said below
- block_slot: int32 [5376], P('band'), may hold values from 0 to 7, as said below
- block_start: int32 [5376], P('band'), may hold values from 0 to 1216, as said below
- lat_weights: float32 [1024], replicated, may hold values from 0.5 to 2
- drag: float32 [16, 2, 1024], P('lev'), may hold values from 0.1 to 1
- mode_inverse: float32 [16, 16], replicated, may hold values from -1.5 to 1.5
- level_modes: float32 [16, 16], replicated, may hold values from -1.5 to 1.5
- depths: float32 [16], replicated, may hold values from 0.1 to 3
Outputs:
- spectral_next: float32 [5376, 16, 128], P('band', 'lev')
Inputs may be any that keep to these rules, and one draw needn't show every extreme that they name: `wave_ids`: distinct wavenumbers. The slots of index b of band, entries b * 8 to (b + 1) * 8 - 1, hold 4 pairs m and 1279 - m in some order; the pair 0 and 1279 is always present. `block_slot`: blocks b * 84 to (b + 1) * 84 - 1 belong to index b of band. For each slot of index b with wavenumber m there is exactly one block with each start 0, 64, 128, ... below 1280 - m, and no other block; the blocks stand in no particular order. `block_start`: A multiple of 64; see block_slot.
All inputs are finite; a program needn't handle non-finite values.
Results may differ from a plain program's by a relative error of at most 0.009.
Values may be sent and summed in bfloat16 or wider, within the bound.
No kernel may reach another device: no remote copies, remote signals or barrier semaphores. Data moves between devices by JAX's collectives and lax.ppermute only.
A program may use at most 128 MiB of HBM per device.

v0:
```python
import math

import jax
import jax.numpy as jnp
from jax import lax
from jax.experimental import pallas as pl
from jax.experimental.pallas import tpu as pltpu
from jax.sharding import PartitionSpec as P

NTRUNC = 1280
NLON = 4096
BLOCKS = 84
ROWS = 64
LATS = 1024
LEVELS = 4
ALL_LEVELS = 16
SOURCES = 64
SENT_ROWS = 24
CHUNK = 12
CHUNKS = BLOCKS // CHUNK
KPAD = 96
XPAD = 1152
XTILES = XPAD // 128
F32 = jnp.float32
BF16 = jnp.bfloat16
MB = 1024 * 1024


def iota(shape, dim):
    return lax.broadcasted_iota(jnp.int32, shape, dim)


def row_offset(lane):
    r = lane % ROWS
    half = ROWS // 2
    return jnp.where(r < half, 2 * r, 2 * (r - half) + 1)


def sincos(turns):
    quarter = ((turns + 512) >> 10) & 3
    rest = ((turns + 512) & 1023) - 512
    t = rest.astype(F32) * (2.0 * math.pi / NLON)
    z = t * t
    s = t * (1.0 + z * (-1.0 / 6 + z * (1.0 / 120 + z * (-1.0 / 5040 + z * (1.0 / 362880)))))
    c = 1.0 + z * (-0.5 + z * (1.0 / 24 + z * (-1.0 / 720 + z * (1.0 / 40320))))
    swap = (quarter & 1) == 1
    cos = jnp.where(swap, s, c)
    sin = jnp.where(swap, c, s)
    cos = jnp.where((quarter == 1) | (quarter == 2), -cos, cos)
    sin = jnp.where(quarter >= 2, -sin, sin)
    return cos, sin


def forward_kernel(
    pos_ref, base_ref, even_ref, lev_ref, spec_ref, mode_ref, leg_ref,
    out_ref, legv_ref, growth_ref, kron_ref, lhs_ref, acc_ref, sems,
):
    copies = [
        pltpu.make_async_copy(
            leg_ref.at[pl.ds(c * CHUNK, CHUNK)], legv_ref.at[pl.ds(c * CHUNK, CHUNK)], sems.at[c]
        )
        for c in range(CHUNKS)
    ]
    for copy in copies:
        copy.start()
    lane = iota((8, 128), 1)
    sub = iota((8, 128), 0)
    offset = row_offset(lane)
    left = lane < 64
    upper = sub < 4
    sign = jnp.where(lane % ROWS < ROWS // 2, 1.0, -1.0).astype(F32)

    def build(j, carry):
        k0 = 2 * j
        degree = jnp.where(upper, base_ref[k0], base_ref[k0 + 1]) + offset
        own = spec_ref[pl.ds(pl.multiple_of(8 * j, 8), 8), :]
        own = jnp.where(degree < NTRUNC, own, 0.0)
        turned = pltpu.roll(own, 64, 1)
        parts = (
            jnp.where(left, own, pltpu.roll(turned, 4, 0)),
            jnp.where(left, turned, pltpu.roll(own, 4, 0)),
        )
        match = jnp.where(left, pos_ref[k0], pos_ref[k0 + 1]) == sub
        where = pl.ds(pl.multiple_of(128 * j, 128), 128)
        for l in range(LEVELS):
            north = jnp.concatenate(
                [
                    jnp.where(match, jnp.broadcast_to(p[l : l + 1], (8, 128)), 0.0)
                    for p in parts
                ],
                axis=0,
            )
            south = north * jnp.concatenate([sign, sign], axis=0)
            lhs_ref[32 * l : 32 * l + 16, where] = north.astype(BF16)
            lhs_ref[32 * l + 16 : 32 * l + 32, where] = south.astype(BF16)
        return carry

    lax.fori_loop(0, BLOCKS // 2, build, 0, unroll=6)

    growth_ref[...] = jnp.zeros_like(growth_ref)
    one = row_offset(iota((1, 128), 1))

    def grow(k, carry):
        degree = (base_ref[k] + one).astype(F32)
        growth_ref[pl.ds(k, 1), :] = degree * (degree + 1.0) / (NTRUNC * NTRUNC)
        return carry

    lax.fori_loop(0, BLOCKS, grow, 0, unroll=12)
    lev = lev_ref[0]
    row_pick = (iota((256, ALL_LEVELS), 0) // 16 == iota((256, ALL_LEVELS), 1)).astype(F32)
    col = iota((ALL_LEVELS, 256), 1) // 16
    source_level = ((lev - col // LEVELS) & 3) * LEVELS + col % LEVELS
    col_pick = (iota((ALL_LEVELS, 256), 0) == source_level).astype(F32)
    high = lax.Precision.HIGHEST
    wide = jnp.dot(jnp.dot(row_pick, mode_ref[...], precision=high), col_pick, precision=high)
    wide = jnp.where(iota((256, 256), 0) % 16 == iota((256, 256), 1) % 16, wide, 0.0)
    wide_high = wide.astype(BF16)
    kron_ref[:, 0:256] = wide_high
    kron_ref[:, 256:512] = (wide - wide_high.astype(F32)).astype(BF16)

    for c in range(CHUNKS):
        copies[c].wait()
        lhs = lhs_ref[:, c * CHUNK * ROWS : (c + 1) * CHUNK * ROWS]
        for n in range(LATS // 256):
            cols = slice(256 * n, 256 * n + 256)
            rhs = legv_ref[c * CHUNK : (c + 1) * CHUNK, :, cols].reshape(CHUNK * ROWS, 256)
            part = jnp.dot(lhs, rhs, preferred_element_type=F32)
            if c == 0:
                acc_ref[:, cols] = part
            else:
                acc_ref[:, cols] += part
    ids = jnp.zeros((8, 128), jnp.int32)
    for p in range(4):
        ids = jnp.where(sub == p, even_ref[p] >> 4, ids)
        ids = jnp.where(sub == 4 + p, even_ref[p] & 15, ids)
    ids = ids.astype(F32).astype(BF16)
    for g in range(8):
        for b in range(8):
            out_ref[8 * g + b, 0:16, :] = acc_ref[
                16 * g : 16 * g + 16, 128 * b : 128 * b + 128
            ].astype(BF16)
            out_ref[8 * g + b, 16:24, :] = ids


def grid_kernel(in_ref, out_ref, recv_ref, tw_ref, g_ref, send_ref):
    recv_ref[...] = in_ref[...].astype(F32).reshape(SOURCES * SENT_ROWS, 128)

    def rows_of(j):
        return recv_ref[pl.ds(j, SOURCES, stride=SENT_ROWS), :]

    lane = iota((32, 128), 1)
    lane8 = iota((8, 128), 1)
    shift = [sincos(((NTRUNC - 1) * (128 * a + lane8)) & (NLON - 1)) for a in range(XTILES)]

    for p in range(4):
        whole = (rows_of(16 + p) * 16.0 + rows_of(20 + p)).astype(jnp.int32)
        for half in range(2):
            wave = whole[32 * half : 32 * half + 32]
            rows = slice(64 * p + 32 * half, 64 * p + 32 * half + 32)
            cos, sin = sincos((wave * lane) & (NLON - 1))
            step_cos, step_sin = sincos((wave * 128) & (NLON - 1))
            for a in range(XTILES):
                cols = slice(128 * a, 128 * a + 128)
                c1 = jnp.concatenate([shift[a][0]] * 4, axis=0)
                s1 = jnp.concatenate([shift[a][1]] * 4, axis=0)
                tw_ref[0, rows, cols] = cos.astype(BF16)
                tw_ref[1, rows, cols] = sin.astype(BF16)
                tw_ref[2, rows, cols] = (c1 * cos + s1 * sin).astype(BF16)
                tw_ref[3, rows, cols] = (s1 * cos - c1 * sin).astype(BF16)
                if a + 1 < XTILES:
                    cos, sin = cos * step_cos - sin * step_sin, sin * step_cos + cos * step_sin

    first_row = (0, 8, 4, 12)
    spectra = [
        jnp.concatenate([rows_of(f + p) for p in range(4)], axis=0).T.astype(BF16)
        for f in first_row
    ]
    for a in range(XTILES):
        cols = slice(128 * a, 128 * a + 128)
        ce, se, co, so = [
            jnp.dot(spectra[i], tw_ref[i, :, cols], preferred_element_type=F32) for i in range(4)
        ]
        minus, plus = ce - se, ce + se
        odd_minus, odd_plus = co - so, co + so
        f1, f2, f3, f4 = [
            v * jnp.abs(v)
            for v in (minus + odd_minus, minus - odd_minus, plus + odd_plus, plus - odd_plus)
        ]
        s12, d12, s34, d34 = f1 + f2, f1 - f2, f3 + f4, f3 - f4
        folded = (s12 + s34, s12 - s34, d12 + d34, d12 - d34)
        if a == 0:
            share = jnp.where(iota((1, 128), 1) == 0, 0.5, 1.0)
        else:
            share = jnp.where(iota((1, 128), 1) == 0, 0.5, 0.0)
        for i in range(4):
            value = folded[i]
            if a in (0, XTILES - 1):
                value = value * share
            g_ref[i, :, cols] = value.astype(BF16)
    scale = 1.0 / (512.0 * 64.0)
    for i in range(4):
        total = lax.dot_general(
            tw_ref[i], g_ref[i], (((1,), (1,)), ((), ())), preferred_element_type=F32
        )
        total = total * (scale if i % 2 == 0 else -scale)
        for p in range(4):
            send_ref[pl.ds(first_row[i] + p, SOURCES, stride=16), :] = total[64 * p : 64 * p + 64]
    out_ref[...] = send_ref[...].reshape(SOURCES, 16, 128).astype(BF16)


def direct_kernel(
    pos_ref, base_ref, arrived_ref, weight_ref, drag_ref, spec_ref, legv_ref,
    out_ref, v_ref, acc_ref, comb_ref,
):
    for b in range(8):
        cols = slice(128 * b, 128 * b + 128)
        weight = -weight_ref[0:1, cols]
        sides = []
        for l in range(LEVELS):
            north = (weight * drag_ref[l, 0:1, cols]) * arrived_ref[16 * l + b].astype(F32)
            south = (weight * drag_ref[l, 1:2, cols]) * arrived_ref[16 * l + 8 + b].astype(F32)
            sides.append((north + south, north - south))
        for a in range(2):
            for c in range(2):
                for pair in range(2):
                    piece = jnp.concatenate(
                        [sides[2 * pair + i][a][8 * c : 8 * c + 8] for i in range(2)], axis=0
                    )
                    row = (a * 2 + c) * 32 + pair * 16
                    v_ref[row : row + 16, cols] = piece.astype(BF16)
    comb_ref[...] = jnp.zeros_like(comb_ref)
    lane = iota((8, 128), 1)
    offset = row_offset(iota((4, 128), 1))
    left = lane < 64
    even_rows = lane % ROWS < ROWS // 2

    def one_group(group, carry):
        rhs = legv_ref[pl.ds(4 * group, 4)].reshape(4 * ROWS, LATS)
        product = lax.dot_general(
            v_ref[...], rhs, (((1,), (1,)), ((), ())), preferred_element_type=F32
        )
        acc_ref[0:128, :] = product[:, 0:128]
        acc_ref[128:256, :] = product[:, 128:256]
        for q in range(4):
            k = 4 * group + q
            rows = acc_ref[pl.ds(128 * (q // 2) + pos_ref[k], 16, stride=8), :]
            value = jnp.where(even_rows, rows[0:8], rows[8:16])
            if q % 2 == 0:
                value = jnp.where(left, value, pltpu.roll(pltpu.roll(value, 64, 1), 4, 0))
            else:
                value = jnp.where(left, pltpu.roll(value, 64, 1), pltpu.roll(value, 4, 0))
            total = value[0:4] + spec_ref[pl.ds(4 * k, 4), :]
            total = jnp.where(base_ref[k] + offset < NTRUNC, total, 0.0)
            comb_ref[pl.ds(k, 4, stride=KPAD), :] = total
        return carry

    lax.fori_loop(0, BLOCKS // 4, one_group, 0, unroll=3)
    out_ref[...] = comb_ref[...].astype(BF16)


def vertical_kernel(
    lev_ref, level_ref, depth_ref, own_ref, one_ref, two_ref, three_ref, growth_ref, kron_ref,
    out_ref,
):
    lev = lev_ref[0]
    sources = (own_ref, one_ref, two_ref, three_ref)
    for t in range(KPAD // 16):
        stacked = jnp.concatenate(
            [
                s[KPAD * j + 16 * t : KPAD * j + 16 * t + 16, :]
                for s in sources
                for j in range(LEVELS)
            ],
            axis=0,
        )
        modal = jnp.dot(kron_ref[:, 0:256], stacked, preferred_element_type=F32) + jnp.dot(
            kron_ref[:, 256:512], stacked, preferred_element_type=F32
        )
        growth = growth_ref[16 * t : 16 * t + 16, :]
        results = [None] * LEVELS
        for a in range(ALL_LEVELS):
            scaled = modal[16 * a : 16 * a + 16] / (1.0 + depth_ref[a] * growth)
            for l in range(LEVELS):
                term = level_ref[lev * LEVELS + l, a] * scaled
                results[l] = term if a == 0 else results[l] + term
        count = min(16, BLOCKS - 16 * t)
        for l in range(LEVELS):
            out_ref[pl.ds(64 * t + l, count, stride=LEVELS), :] = results[l][0:count]


def specs(*kinds):
    spaces = {"s": pltpu.SMEM, "v": pltpu.VMEM, "h": pl.ANY}
    return [pl.BlockSpec(memory_space=spaces[k]) for k in kinds]


def on_device(
    spectral, legendre, wave_ids, block_slot, block_start, lat_weights, drag, mode_inverse,
    level_modes, depths,
):
    odd = wave_ids % 2
    key = jnp.where(odd == 1, NTRUNC + (NTRUNC - 1 - wave_ids), wave_ids)
    place = jnp.sum((key[None, :] < key[:, None]).astype(jnp.int32), axis=1)
    slots = jnp.arange(8, dtype=jnp.int32)
    match = block_slot[:, None] == slots[None, :]
    pos = jnp.sum(jnp.where(match, place[None, :], 0), axis=1)
    base = jnp.sum(jnp.where(match, wave_ids[None, :], 0), axis=1) + block_start
    evens = jnp.sum(jnp.where(place[None, :] == slots[:4, None], wave_ids[None, :], 0), axis=1)
    lev = lax.axis_index("lev").astype(jnp.int32).reshape(1)
    spec = spectral.reshape(BLOCKS * LEVELS, 128)

    outgoing, legv, growth, kron = pl.pallas_call(
        forward_kernel,
        in_specs=specs("s", "s", "s", "s", "v", "v", "h"),
        out_specs=specs("v", "v", "v", "v"),
        out_shape=(
            jax.ShapeDtypeStruct((SOURCES, SENT_ROWS, 128), BF16),
            pltpu.VMEM((BLOCKS, ROWS, LATS), BF16),
            jax.ShapeDtypeStruct((KPAD, 128), F32),
            jax.ShapeDtypeStruct((256, 512), BF16),
        ),
        scratch_shapes=[
            pltpu.VMEM((128, BLOCKS * ROWS), BF16),
            pltpu.VMEM((128, LATS), F32),
            pltpu.SemaphoreType.DMA((CHUNKS,)),
        ],
        compiler_params=pltpu.CompilerParams(vmem_limit_bytes=32 * MB),
        name="forward",
    )(pos, base, evens, lev, spec, mode_inverse, legendre)
    incoming = lax.all_to_all(outgoing, "band", split_axis=0, concat_axis=0, tiled=True)
    filtered = pl.pallas_call(
        grid_kernel,
        in_specs=specs("v"),
        out_specs=specs("v")[0],
        out_shape=jax.ShapeDtypeStruct((SOURCES, 16, 128), BF16),
        scratch_shapes=[
            pltpu.VMEM((SOURCES * SENT_ROWS, 128), F32),
            pltpu.VMEM((4, 256, XPAD), BF16),
            pltpu.VMEM((4, 128, XPAD), BF16),
            pltpu.VMEM((SOURCES * 16, 128), F32),
        ],
        compiler_params=pltpu.CompilerParams(vmem_limit_bytes=24 * MB),
        name="grid",
    )(incoming)
    arrived = lax.all_to_all(filtered, "band", split_axis=0, concat_axis=0, tiled=True)
    combined = pl.pallas_call(
        direct_kernel,
        in_specs=specs("s", "s", "v", "v", "v", "v", "v"),
        out_specs=specs("v")[0],
        out_shape=jax.ShapeDtypeStruct((LEVELS * KPAD, 128), BF16),
        scratch_shapes=[
            pltpu.VMEM((128, LATS), BF16),
            pltpu.VMEM((256, 128), F32),
            pltpu.VMEM((LEVELS * KPAD, 128), F32),
        ],
        compiler_params=pltpu.CompilerParams(vmem_limit_bytes=32 * MB),
        name="direct",
    )(pos, base, arrived, lat_weights.reshape(1, LATS), drag, spec, legv)
    others = [
        lax.ppermute(combined, "lev", [(i, (i + s) % 4) for i in range(4)]) for s in (1, 2, 3)
    ]
    result = pl.pallas_call(
        vertical_kernel,
        in_specs=specs("s", "s", "s", "v", "v", "v", "v", "v", "v"),
        out_specs=specs("v")[0],
        out_shape=jax.ShapeDtypeStruct((BLOCKS * LEVELS, 128), F32),
        compiler_params=pltpu.CompilerParams(vmem_limit_bytes=16 * MB),
        name="vertical",
    )(lev, level_modes, depths, combined, *others, growth, kron)
    return result.reshape(BLOCKS, LEVELS, 128)


def solution(mesh):
    placed = (
        P("band", "lev", None),
        P("band", None, None),
        P("band"),
        P("band"),
        P("band"),
        P(),
        P("lev", None, None),
        P(),
        P(),
        P(),
    )
    return jax.shard_map(
        on_device, mesh=mesh, in_specs=placed, out_specs=P("band", "lev", None), check_vma=False
    )
```

profile of v0, /device:TPU:1, one launch (start us, length us, event | category | flops | bytes accessed | tf_op | source)
XLA Modules:
  0.0 81.9 jit_solution(13602128842601893567)
XLA Ops:
  0.0 0.0 copy-start.6
  0.0 0.7 compare_select_fusion.2
  0.7 0.2 convert_reduce_fusion
  0.9 0.8 %select_reduce_fusion.2.even_ref = s32[4]{0:T(128)S(1)} fusion(s32[8]{0:T(128)} %param.12, s32[8]{0:T(128)S(1)} %convert_reduce_fusion, s32[4]{0:T(128)S(1)} %bitcast.8), kind=kLoop, calls=%fused_computation.6 | loop fusion | flops 92 | bytes 96 | tf_op jit(solution)/shard_map/reduce_sum | solution.py:307
  1.7 0.8 select_reduce_fusion
  2.5 0.7 add.18.base_ref
  3.1 0.0 copy-start
  3.1 4.1 %copy-done = bf16[84,64,1024]{2,1,0:T(8,128)(2,1)S(1)} copy-done((bf16[84,64,1024]{2,1,0:T(8,128)(2,1)S(1)}, bf16[84,64,1024]{2,1,0:T(8,128)(2,1)}, u32[]{:S(2)}) %copy-start) | copy-done | bytes 11010072
  7.3 0.0 copy-start.1
  7.3 0.9 %copy-done.1 = f32[84,4,128]{2,1,0:T(4,128)S(1)} copy-done((f32[84,4,128]{2,1,0:T(4,128)S(1)}, f32[84,4,128]{2,1,0:T(4,128)}, u32[]{:S(2)}) %copy-start.1) | copy-done | bytes 172056
  8.2 0.0 copy-start.4
  8.2 0.7 copy-done.4
  8.9 0.0 copy-start.2
  8.9 0.0 copy-start.3
  8.9 0.0 copy-start.5
  8.9 0.0 copy-start.7
  8.9 5.7 %forward.1 = (bf16[64,24,128]{2,1,0:T(8,128)(2,1)S(1)}, bf16[84,64,1024]{2,1,0:T(8,128)(2,1)S(1)}, f32[96,128]{1,0:T(8,128)S(1)}, bf16[256,512]{1,0:T(8,128)(2,1)S(1)}) custom-call(s32[84]{0:T(128)S(1)} %get-tuple-element.14.pos_ref, s32[84]{0:T(128)S(1)} %add.18.base_ref, s32[4]{0:T(128)S(1)} %select_reduce_fusion.2.even_ref, s32[1]{0:T(128)} %bitcast.lev_ref, ...), custom_call_target="tpu_custom_call" | custom-call | tf_op jit(solution)/shard_map/forward/pallas_call | solution.py:311
  14.6 27.5 %all_to_all.10.in_ref = bf16[64,24,128]{2,1,0:T(8,128)(2,1)S(1)} all-to-all(bf16[64,24,128]{2,1,0:T(8,128)(2,1)S(1)} %get-tuple-element.9), channel_id=1, replica_groups=mesh['band'=64,'lev'=4] {'band'}, dimensions={0} | all-to-all | bytes 786432 | tf_op jit(solution)/shard_map/all_to_all | solution.py:329
  42.1 3.4 %grid.1 = bf16[64,16,128]{2,1,0:T(8,128)(2,1)S(1)} custom-call(bf16[64,24,128]{2,1,0:T(8,128)(2,1)S(1)} %all_to_all.10.in_ref), custom_call_target="tpu_custom_call" | custom-call | tf_op jit(solution)/shard_map/grid/pallas_call | solution.py:330
  45.4 18.0 %all_to_all.11.arrived_ref = bf16[64,16,128]{2,1,0:T(8,128)(2,1)S(1)} all-to-all(bf16[64,16,128]{2,1,0:T(8,128)(2,1)S(1)} %grid.1), channel_id=1, replica_groups=mesh['band'=64,'lev'=4] {'band'}, dimensions={0} | all-to-all | bytes 524288 | tf_op jit(solution)/shard_map/all_to_all | solution.py:344
  63.4 0.0 copy-done.6
  63.4 0.0 copy-done.2
  63.4 0.0 copy-done.3
  63.4 5.9 %direct.1.own_ref = bf16[384,128]{1,0:T(8,128)(2,1)S(1)} custom-call(s32[84]{0:T(128)S(1)} %get-tuple-element.14.pos_ref, s32[84]{0:T(128)S(1)} %add.18.base_ref, bf16[64,16,128]{2,1,0:T(8,128)(2,1)S(1)} %all_to_all.11.arrived_ref, f32[1,1024]{1,0:T(1,128)S(1)} %bitcast.7, f32[4,2,1024]{2,1,0:T(2,128)S(1)} %copy-done.3, f32[336,128]{1,0:T(8,128)S(1)} %bitcast.6, ...), custom_call_target="tpu_custom_call" | custom-call | tf_op jit(solution)/shard_map/direct/pallas_call | solution.py:345
  69.4 2.6 %collective-permute-start.2 = (bf16[384,128]{1,0:T(8,128)(2,1)S(1)}, bf16[384,128]{1,0:T(8,128)(2,1)S(1)}, u32[]{:S(2)}, u32[]{:S(2)}) collective-permute-start(bf16[384,128]{1,0:T(8,128)(2,1)S(1)} %direct.1.own_ref), channel_id=1, source_target_pairs={{0,3},{1,0},{2,1},{3,2},{4,7},{5,4},{6,5},{7,6},{8,11},{9,8},{10,9... | collective-permute-start | bytes 294920 | tf_op jit(solution)/shard_map/ppermute | solution.py:359
  71.9 0.5 collective-permute-start.1
  72.5 0.6 collective-permute-start
  73.1 0.5 collective-permute-done.2.three_ref
  73.6 3.4 %collective-permute-done.1.two_ref = bf16[384,128]{1,0:T(8,128)(2,1)S(1)} collective-permute-done((bf16[384,128]{1,0:T(8,128)(2,1)S(1)}, bf16[384,128]{1,0:T(8,128)(2,1)S(1)}, u32[]{:S(2)}, u32[]{:S(2)}) %collective-permute-start.1) | collective-permute-done | bytes 98336 | tf_op jit(solution)/shard_map/ppermute | solution.py:359
  77.0 3.0 %collective-permute-done.one_ref = bf16[384,128]{1,0:T(8,128)(2,1)S(1)} collective-permute-done((bf16[384,128]{1,0:T(8,128)(2,1)S(1)}, bf16[384,128]{1,0:T(8,128)(2,1)S(1)}, u32[]{:S(2)}, u32[]{:S(2)}) %collective-permute-start) | collective-permute-done | bytes 98336 | tf_op jit(solution)/shard_map/ppermute | solution.py:359
  80.0 0.0 copy-done.5
  80.0 0.0 copy-done.7
  80.0 2.0 %vertical.1 = f32[336,128]{1,0:T(8,128)} custom-call(s32[1]{0:T(128)} %bitcast.lev_ref, f32[16,16]{1,0:T(8,128)S(1)} %copy-done.5, f32[16]{0:T(128)S(1)} %copy-done.7, bf16[384,128]{1,0:T(8,128)(2,1)S(1)} %direct.1.own_ref, bf16[384,128]{1,0:T(8,128)(2,1)S(1)} %collective-permute-done.one_ref, bf16[384,128]{1,0:T(8,128)(2,1)S(1)} %collective-permute-done.1.two_ref, ...), custom_call_target="tpu_custom_call" | custom-call | tf_op jit(solution)/shard_map/vertical/pallas_call | solution.py:361
  (1 shorter events, 0.0 us)
Async XLA Ops:
  0.0 63.4 %copy-start.6 = (f32[1024]{0:T(1024)S(1)}, f32[1024]{0:T(1024)}, u32[]{:S(2)}) copy-start(f32[1024]{0:T(1024)} %param.15) | copy-start | bytes 12292
  3.1 4.1 %copy-start = (bf16[84,64,1024]{2,1,0:T(8,128)(2,1)S(1)}, bf16[84,64,1024]{2,1,0:T(8,128)(2,1)}, u32[]{:S(2)}) copy-start(bf16[84,64,1024]{2,1,0:T(8,128)(2,1)} %leg_ref.1) | copy-start | bytes 33030148
  7.3 0.9 %copy-start.1 = (f32[84,4,128]{2,1,0:T(4,128)S(1)}, f32[84,4,128]{2,1,0:T(4,128)}, u32[]{:S(2)}) copy-start(f32[84,4,128]{2,1,0:T(4,128)} %param.10) | copy-start | bytes 516100
  8.2 0.7 copy-start.4
  8.9 54.6 %copy-start.2 = (f32[84,4,128]{2,1,0:T(4,128)S(1)}, f32[84,4,128]{2,1,0:T(4,128)}, u32[]{:S(2)}) copy-start(f32[84,4,128]{2,1,0:T(4,128)} %param.10) | copy-start | bytes 516100
  8.9 54.6 %copy-start.3 = (f32[4,2,1024]{2,1,0:T(2,128)S(1)}, f32[4,2,1024]{2,1,0:T(2,128)}, u32[]{:S(2)}) copy-start(f32[4,2,1024]{2,1,0:T(2,128)} %drag_ref.1) | copy-start | bytes 98308
  8.9 71.1 %copy-start.5 = (f32[16,16]{1,0:T(8,128)S(1)}, f32[16,16]{1,0:T(8,128)}, u32[]{:S(2)}) copy-start(f32[16,16]{1,0:T(8,128)} %level_ref.1) | copy-start | bytes 3076
  8.9 71.1 %copy-start.7 = (f32[16]{0:T(128)S(1)}, f32[16]{0:T(128)}, u32[]{:S(2)}) copy-start(f32[16]{0:T(128)} %depth_ref.1) | copy-start | bytes 196
  69.4 4.2 %collective-permute-start.2 = (bf16[384,128]{1,0:T(8,128)(2,1)S(1)}, bf16[384,128]{1,0:T(8,128)(2,1)S(1)}, u32[]{:S(2)}, u32[]{:S(2)}) collective-permute-start(bf16[384,128]{1,0:T(8,128)(2,1)S(1)} %direct.1.own_ref), channel_id=1, source_target_pairs={{0,3},{1,0},{2,1},{3,2},{4,7},{5,4},{6,5},{7,6},{8,11},{9,8},{10,9... | collective-permute-start | bytes 294920 | tf_op jit(solution)/shard_map/ppermute | solution.py:359
  71.9 5.1 %collective-permute-start.1 = (bf16[384,128]{1,0:T(8,128)(2,1)S(1)}, bf16[384,128]{1,0:T(8,128)(2,1)S(1)}, u32[]{:S(2)}, u32[]{:S(2)}) collective-permute-start(bf16[384,128]{1,0:T(8,128)(2,1)S(1)} %direct.1.own_ref), channel_id=1, source_target_pairs={{0,2},{1,3},{2,0},{3,1},{4,6},{5,7},{6,4},{7,5},{8,10},{9,11},{10,... | collective-permute-start | bytes 294920 | tf_op jit(solution)/shard_map/ppermute | solution.py:359
  72.5 7.5 %collective-permute-start = (bf16[384,128]{1,0:T(8,128)(2,1)S(1)}, bf16[384,128]{1,0:T(8,128)(2,1)S(1)}, u32[]{:S(2)}, u32[]{:S(2)}) collective-permute-start(bf16[384,128]{1,0:T(8,128)(2,1)S(1)} %direct.1.own_ref), channel_id=1, source_target_pairs={{0,1},{1,2},{2,3},{3,0},{4,5},{5,6},{6,7},{7,4},{8,9},{9,10},{10,1... | collective-permute-start | bytes 294920 | tf_op jit(solution)/shard_map/ppermute | solution.py:359
where the time goes:
time: 82.2 us; the launch traced here: 81.9 us
  blocking collectives  45.5 us (55%)
  Pallas kernels  16.9 us (21%)
  waiting for transfers between devices  6.89 us (8%)
  local copies, waits for them, and re-layouts  5.76 us (7%)
  starting transfers between devices  3.68 us (4%)
  other arithmetic  3.11 us (4%)
    all_to_all x1, blocking collectives, on_device(): lax.all_to_all(outgoing, 'band', split_axis=0, concat_axis=0, tiled=True)  27.5 us
    all_to_all x1, blocking collectives, on_device(): lax.all_to_all(filtered, 'band', split_axis=0, concat_axis=0, tiled=True)  18 us
    ppermute x3, waiting for transfers between devices, on_device(): lax.ppermute(combined, 'lev', [(i, (i + s) % 4) for i in range(4)])  6.89 us
    pallas_call x1, Pallas kernels, on_device(): pl.pallas_call(direct_kernel, in_specs=specs('s', 's', 'v', 'v', 'v', 'v'...  5.92 us
    unnamed x16, local copies, waits for them, and re-layouts  5.76 us
    pallas_call x1, Pallas kernels, on_device(): pl.pallas_call(forward_kernel, in_specs=specs('s', 's', 's', 's', 'v', 'v...  5.67 us
    ppermute x3, starting transfers between devices, on_device(): lax.ppermute(combined, 'lev', [(i, (i + s) % 4) for i in range(4)])  3.68 us
    pallas_call x1, Pallas kernels, on_device(): pl.pallas_call(grid_kernel, in_specs=specs('v'), out_specs=specs('v')[0],...  3.37 us
  transfers between devices with their start and end apart: 3, of which 3 were waited for; matrix products, arithmetic and copies ran while one was open for 0% of the time, Pallas kernels for 0%

commit v1 on v0

v1 whole, which is shorter than its diff:
```python
import math

import jax
import jax.numpy as jnp
from jax import lax
from jax.experimental import pallas as pl
from jax.experimental.pallas import tpu as pltpu
from jax.sharding import PartitionSpec as P

NTRUNC = 1280
NLON = 4096
BLOCKS = 84
ROWS = 64
LATS = 1024
LEVELS = 4
ALL_LEVELS = 16
SOURCES = 64
SENT_ROWS = 18
CHUNK = 12
CHUNKS = BLOCKS // CHUNK
KPAD = 88
XPAD = 1152
XTILES = XPAD // 128
F32 = jnp.float32
BF16 = jnp.bfloat16
MB = 1024 * 1024


def iota(shape, dim):
    return lax.broadcasted_iota(jnp.int32, shape, dim)


def row_offset(lane):
    r = lane % ROWS
    half = ROWS // 2
    return jnp.where(r < half, 2 * r, 2 * (r - half) + 1)


def sincos(turns):
    quarter = ((turns + 512) >> 10) & 3
    rest = ((turns + 512) & 1023) - 512
    t = rest.astype(F32) * (2.0 * math.pi / NLON)
    z = t * t
    s = t * (1.0 + z * (-1.0 / 6 + z * (1.0 / 120 + z * (-1.0 / 5040 + z * (1.0 / 362880)))))
    c = 1.0 + z * (-0.5 + z * (1.0 / 24 + z * (-1.0 / 720 + z * (1.0 / 40320))))
    swap = (quarter & 1) == 1
    cos = jnp.where(swap, s, c)
    sin = jnp.where(swap, c, s)
    cos = jnp.where((quarter == 1) | (quarter == 2), -cos, cos)
    sin = jnp.where(quarter >= 2, -sin, sin)
    return cos, sin


def forward_kernel(
    wave_hbm, slot_hbm, start_hbm, spec_hbm, leg_hbm,
    out_ref, legv_ref, masked_ref, pos_hbm, base_hbm,
    wave_ref, slot_ref, start_ref, place_ref, pos_ref, base_ref, lhs_ref, acc_ref, send_ref,
    sems, small,
):
    inputs = [
        pltpu.make_async_copy(wave_hbm, wave_ref, small.at[0]),
        pltpu.make_async_copy(slot_hbm, slot_ref, small.at[1]),
        pltpu.make_async_copy(start_hbm, start_ref, small.at[2]),
        pltpu.make_async_copy(spec_hbm, masked_ref, small.at[3]),
    ]
    for copy in inputs:
        copy.start()
    copies = [
        pltpu.make_async_copy(
            leg_hbm.at[pl.ds(c * CHUNK, CHUNK)], legv_ref.at[pl.ds(c * CHUNK, CHUNK)], sems.at[c]
        )
        for c in range(CHUNKS)
    ]
    for copy in copies:
        copy.start()
    for copy in inputs:
        copy.wait()
    lane = iota((8, 128), 1)
    sub = iota((8, 128), 0)
    offset = row_offset(lane)
    left = lane < 64
    upper = sub < 4
    sign = jnp.where(lane % ROWS < ROWS // 2, 1.0, -1.0).astype(F32)

    waves = [wave_ref[s] for s in range(8)]
    keys = [jnp.where(w % 2 == 1, 2 * NTRUNC - 1 - w, w) for w in waves]
    places = []
    for s in range(8):
        place = jnp.int32(0)
        for other in range(8):
            if other != s:
                place = place + (keys[other] < keys[s]).astype(jnp.int32)
        place_ref[s] = place
        places.append(place)
    ids = jnp.zeros((8, 128), jnp.int32)
    for s in range(8):
        ids = jnp.where(lane // 32 == places[s], waves[s], ids)
    ids = jnp.where(sub == 0, ids >> 4, ids & 15).astype(F32)

    def index(k, carry):
        slot = slot_ref[k]
        pos_ref[k] = place_ref[slot]
        base_ref[k] = wave_ref[slot] + start_ref[k]
        return carry

    lax.fori_loop(0, BLOCKS, index, 0, unroll=12)
    results = [
        pltpu.make_async_copy(pos_ref, pos_hbm, small.at[4]),
        pltpu.make_async_copy(base_ref, base_hbm, small.at[5]),
    ]
    for copy in results:
        copy.start()

    def build(j, carry):
        k0 = 2 * j
        degree = jnp.where(upper, base_ref[k0], base_ref[k0 + 1]) + offset
        here = pl.ds(pl.multiple_of(8 * j, 8), 8)
        own = jnp.where(degree < NTRUNC, masked_ref[here, :], 0.0)
        masked_ref[here, :] = own
        turned = pltpu.roll(own, 64, 1)
        parts = (
            jnp.where(left, own, pltpu.roll(turned, 4, 0)),
            jnp.where(left, turned, pltpu.roll(own, 4, 0)),
        )
        match = jnp.where(left, pos_ref[k0], pos_ref[k0 + 1]) == sub
        for l in range(LEVELS):
            north = jnp.concatenate(
                [
                    jnp.where(match, jnp.broadcast_to(p[l : l + 1], (8, 128)), 0.0)
                    for p in parts
                ],
                axis=0,
            )
            south = north * jnp.concatenate([sign, sign], axis=0)
            lhs_ref[j, 32 * l : 32 * l + 16, :] = north.astype(BF16)
            lhs_ref[j, 32 * l + 16 : 32 * l + 32, :] = south.astype(BF16)
        return carry

    lax.fori_loop(0, BLOCKS // 2, build, 0, unroll=6)

    half = CHUNK // 2
    for c in range(CHUNKS):
        copies[c].wait()
        lhs = jnp.concatenate([lhs_ref[c * half + i] for i in range(half)], axis=1)
        for n in range(LATS // 256):
            rhs = legv_ref[c * CHUNK : (c + 1) * CHUNK, :, 256 * n : 256 * n + 256]
            part = jnp.dot(lhs, rhs.reshape(CHUNK * ROWS, 256), preferred_element_type=F32)
            for i in range(2):
                b = 2 * n + i
                piece = part[:, 128 * i : 128 * i + 128]
                if c > 0:
                    piece = piece + acc_ref[b]
                if c + 1 < CHUNKS:
                    acc_ref[b] = piece
                else:
                    for g in range(8):
                        row = SENT_ROWS * (8 * g + b)
                        send_ref[row : row + 16, :] = piece[16 * g : 16 * g + 16]
                        send_ref[row + 16 : row + 18, :] = ids[0:2]
    out_ref[...] = send_ref[...].astype(BF16)
    for copy in results:
        copy.wait()


def prepare_kernel(
    lev_ref, base_ref, level_ref, depth_ref, mode_ref,
    gain_ref, kron_ref, coef_ref, growth_ref,
):
    lev = lev_ref[0]
    row_pick = (iota((128, ALL_LEVELS), 0) // 8 == iota((128, ALL_LEVELS), 1)).astype(F32)
    col = iota((ALL_LEVELS, 128), 1) // 8
    source_level = ((lev - col // LEVELS) & 3) * LEVELS + col % LEVELS
    col_pick = (iota((ALL_LEVELS, 128), 0) == source_level).astype(F32)
    high = lax.Precision.HIGHEST
    wide = jnp.dot(jnp.dot(row_pick, mode_ref[...], precision=high), col_pick, precision=high)
    wide = jnp.where(iota((128, 128), 0) % 8 == iota((128, 128), 1) % 8, wide, 0.0)
    wide_high = wide.astype(BF16)
    kron_ref[0] = wide_high
    kron_ref[1] = (wide - wide_high.astype(F32)).astype(BF16)

    growth_ref[...] = jnp.zeros_like(growth_ref)
    one = row_offset(iota((1, 128), 1))

    def grow(k, carry):
        degree = (base_ref[k] + one).astype(F32)
        growth_ref[pl.ds(k, 1), :] = degree * (degree + 1.0) / (NTRUNC * NTRUNC)
        return carry

    lax.fori_loop(0, BLOCKS, grow, 0, unroll=12)
    for a in range(ALL_LEVELS):
        gain_ref[a] = 1.0 / (1.0 + depth_ref[a] * growth_ref[...])
        for l in range(LEVELS):
            coef_ref[16 * l + a : 16 * l + a + 1, :] = jnp.full(
                (1, 128), level_ref[lev * LEVELS + l, a], F32
            )


def grid_kernel(in_ref, out_ref, recv_ref, tw_ref, g_ref, send_ref):
    recv_ref[...] = in_ref[...].astype(F32)

    def rows_of(j):
        return recv_ref[pl.ds(j, SOURCES, stride=SENT_ROWS), :]

    lane = iota((32, 128), 1)
    lane8 = iota((8, 128), 1)
    shift = [sincos(((NTRUNC - 1) * (128 * a + lane8)) & (NLON - 1)) for a in range(XTILES)]
    ids = rows_of(16) * 16.0 + rows_of(17)

    for p in range(4):
        whole = jnp.broadcast_to(ids[:, 32 * p : 32 * p + 1], (SOURCES, 128)).astype(jnp.int32)
        for half in range(2):
            wave = whole[32 * half : 32 * half + 32]
            rows = slice(64 * p + 32 * half, 64 * p + 32 * half + 32)
            cos, sin = sincos((wave * lane) & (NLON - 1))
            step_cos, step_sin = sincos((wave * 128) & (NLON - 1))
            for a in range(XTILES):
                c1 = jnp.concatenate([shift[a][0]] * 4, axis=0)
                s1 = jnp.concatenate([shift[a][1]] * 4, axis=0)
                tw_ref[0, a, rows, :] = cos.astype(BF16)
                tw_ref[1, a, rows, :] = sin.astype(BF16)
                tw_ref[2, a, rows, :] = (c1 * cos + s1 * sin).astype(BF16)
                tw_ref[3, a, rows, :] = (s1 * cos - c1 * sin).astype(BF16)
                if a + 1 < XTILES:
                    cos, sin = cos * step_cos - sin * step_sin, sin * step_cos + cos * step_sin

    first_row = (0, 8, 4, 12)
    spectra = [
        jnp.concatenate([rows_of(f + p) for p in range(4)], axis=0).T.astype(BF16)
        for f in first_row
    ]
    for a in range(XTILES):
        ce, se, co, so = [
            jnp.dot(spectra[i], tw_ref[i, a], preferred_element_type=F32) for i in range(4)
        ]
        minus, plus = ce - se, ce + se
        odd_minus, odd_plus = co - so, co + so
        f1, f2, f3, f4 = [
            v * jnp.abs(v)
            for v in (minus + odd_minus, minus - odd_minus, plus + odd_plus, plus - odd_plus)
        ]
        s12, d12, s34, d34 = f1 + f2, f1 - f2, f3 + f4, f3 - f4
        folded = (s12 + s34, s12 - s34, d12 + d34, d12 - d34)
        if a == 0:
            share = jnp.where(iota((1, 128), 1) == 0, 0.5, 1.0)
        else:
            share = jnp.where(iota((1, 128), 1) == 0, 0.5, 0.0)
        for i in range(4):
            value = folded[i]
            if a in (0, XTILES - 1):
                value = value * share
            g_ref[i, a] = value.astype(BF16)
    scale = 1.0 / (512.0 * 64.0)
    for i in range(4):
        total = lax.dot_general(
            jnp.concatenate([tw_ref[i, a] for a in range(XTILES)], axis=1),
            jnp.concatenate([g_ref[i, a] for a in range(XTILES)], axis=1),
            (((1,), (1,)), ((), ())),
            preferred_element_type=F32,
        )
        total = total * (scale if i % 2 == 0 else -scale)
        for p in range(4):
            send_ref[pl.ds(first_row[i] + p, SOURCES, stride=16), :] = total[64 * p : 64 * p + 64]
    out_ref[...] = send_ref[...].reshape(SOURCES, 16, 128).astype(BF16)


def direct_kernel(
    pos_hbm, base_hbm, arrived_ref, weight_ref, drag_ref, masked_ref, legv_ref,
    out_ref, pos_ref, base_ref, v_ref, acc_ref, comb_ref, small,
):
    inputs = [
        pltpu.make_async_copy(pos_hbm, pos_ref, small.at[0]),
        pltpu.make_async_copy(base_hbm, base_ref, small.at[1]),
    ]
    for copy in inputs:
        copy.start()
    for b in range(8):
        cols = slice(128 * b, 128 * b + 128)
        weight = -weight_ref[0:1, cols]
        sides = []
        for l in range(LEVELS):
            north = (weight * drag_ref[l, 0:1, cols]) * arrived_ref[16 * l + b].astype(F32)
            south = (weight * drag_ref[l, 1:2, cols]) * arrived_ref[16 * l + 8 + b].astype(F32)
            sides.append((north + south, north - south))
        for a in range(2):
            for c in range(2):
                for pair in range(2):
                    piece = jnp.concatenate(
                        [sides[2 * pair + i][a][8 * c : 8 * c + 8] for i in range(2)], axis=0
                    )
                    row = (a * 2 + c) * 32 + pair * 16
                    v_ref[b, row : row + 16, :] = piece.astype(BF16)
    comb_ref[...] = jnp.zeros_like(comb_ref)
    lane = iota((8, 128), 1)
    offset = row_offset(iota((4, 128), 1))
    left = lane < 64
    even_rows = lane % ROWS < ROWS // 2
    for copy in inputs:
        copy.wait()

    def finish(group, part, product):
        acc_ref[part, 0:128, :] = product[:, 0:128]
        acc_ref[part, 128:256, :] = product[:, 128:256]
        for q in range(4):
            k = 4 * group + q
            rows = acc_ref[part, pl.ds(128 * (q // 2) + pos_ref[k], 16, stride=8), :]
            value = jnp.where(even_rows, rows[0:8], rows[8:16])
            if q % 2 == 0:
                value = jnp.where(left, value, pltpu.roll(pltpu.roll(value, 64, 1), 4, 0))
            else:
                value = jnp.where(left, pltpu.roll(value, 64, 1), pltpu.roll(value, 4, 0))
            live = base_ref[k] + offset < NTRUNC
            total = jnp.where(live, value[0:4] + masked_ref[pl.ds(4 * k, 4), :], 0.0)
            comb_ref[pl.ds(k, 4, stride=KPAD), :] = total

    def groups_of(step, carry):
        lhs = jnp.concatenate([v_ref[b] for b in range(8)], axis=1)
        for part in range(3):
            group = 3 * step + part
            rhs = legv_ref[pl.ds(4 * group, 4)].reshape(4 * ROWS, LATS)
            product = lax.dot_general(
                lhs, rhs, (((1,), (1,)), ((), ())), preferred_element_type=F32
            )
            finish(group, part, product)
        return carry

    lax.fori_loop(0, BLOCKS // 12, groups_of, 0)
    out_ref[...] = comb_ref[...].astype(BF16)


def vertical_kernel(
    own_ref, one_ref, two_ref, three_ref, gain_ref, kron_ref, coef_ref,
    out_hbm, out_ref, sems,
):
    sources = (own_ref, one_ref, two_ref, three_ref)
    both = jnp.concatenate([kron_ref[0], kron_ref[1]], axis=1)
    copies = []
    for t in range(KPAD // 8):
        stacked = jnp.concatenate(
            [
                s[KPAD * j + 8 * t : KPAD * j + 8 * t + 8, :]
                for s in sources
                for j in range(LEVELS)
            ],
            axis=0,
        )
        modal = jnp.dot(
            both, jnp.concatenate([stacked, stacked], axis=0), preferred_element_type=F32
        )
        results = [None] * LEVELS
        for a in range(ALL_LEVELS):
            scaled = modal[8 * a : 8 * a + 8] * gain_ref[a, 8 * t : 8 * t + 8, :]
            for l in range(LEVELS):
                term = coef_ref[16 * l + a : 16 * l + a + 1, :] * scaled
                results[l] = term if a == 0 else results[l] + term
        count = min(8, BLOCKS - 8 * t)
        for l in range(LEVELS):
            out_ref[pl.ds(32 * t + l, count, stride=LEVELS), :] = results[l][0:count]
        rows = pl.ds(32 * t, 4 * count)
        copies.append(pltpu.make_async_copy(out_ref.at[rows], out_hbm.at[rows], sems.at[t]))
        copies[-1].start()
    for copy in copies:
        copy.wait()


def specs(*kinds):
    spaces = {"s": pltpu.SMEM, "v": pltpu.VMEM, "h": pltpu.HBM, "a": pl.ANY}
    return [pl.BlockSpec(memory_space=spaces[k]) for k in kinds]


def in_hbm(x):
    return pltpu.with_memory_space_constraint(x, pltpu.HBM)


def on_device(
    spectral, legendre, wave_ids, block_slot, block_start, lat_weights, drag, mode_inverse,
    level_modes, depths,
):
    lev = lax.axis_index("lev").astype(jnp.int32).reshape(1)
    spec = spectral.reshape(BLOCKS * LEVELS, 128)
    outgoing, legv, masked, pos, base = pl.pallas_call(
        forward_kernel,
        in_specs=specs("h", "h", "h", "h", "h"),
        out_specs=specs("v", "v", "v", "h", "h"),
        out_shape=(
            jax.ShapeDtypeStruct((SOURCES * SENT_ROWS, 128), BF16),
            pltpu.VMEM((BLOCKS, ROWS, LATS), BF16),
            pltpu.VMEM((BLOCKS * LEVELS, 128), F32),
            jax.ShapeDtypeStruct((BLOCKS,), jnp.int32),
            jax.ShapeDtypeStruct((BLOCKS,), jnp.int32),
        ),
        scratch_shapes=[
            pltpu.SMEM((8,), jnp.int32),
            pltpu.SMEM((BLOCKS,), jnp.int32),
            pltpu.SMEM((BLOCKS,), jnp.int32),
            pltpu.SMEM((8,), jnp.int32),
            pltpu.SMEM((BLOCKS,), jnp.int32),
            pltpu.SMEM((BLOCKS,), jnp.int32),
            pltpu.VMEM((BLOCKS // 2, 128, 128), BF16),
            pltpu.VMEM((8, 128, 128), F32),
            pltpu.VMEM((SOURCES * SENT_ROWS, 128), F32),
            pltpu.SemaphoreType.DMA((CHUNKS,)),
            pltpu.SemaphoreType.DMA((6,)),
        ],
        compiler_params=pltpu.CompilerParams(vmem_limit_bytes=24 * MB),
        name="forward",
    )(*[in_hbm(x) for x in (wave_ids, block_slot, block_start, spec, legendre)])
    pairs = SENT_ROWS // 2
    incoming = lax.all_to_all(
        outgoing.reshape(SOURCES, pairs, 2, 128), "band", split_axis=0, concat_axis=0, tiled=True
    ).reshape(SOURCES * SENT_ROWS, 128)
    filtered = pl.pallas_call(
        grid_kernel,
        in_specs=specs("v"),
        out_specs=specs("v")[0],
        out_shape=jax.ShapeDtypeStruct((SOURCES, 16, 128), BF16),
        scratch_shapes=[
            pltpu.VMEM((SOURCES * SENT_ROWS, 128), F32),
            pltpu.VMEM((4, XTILES, 256, 128), BF16),
            pltpu.VMEM((4, XTILES, 128, 128), BF16),
            pltpu.VMEM((SOURCES * 16, 128), F32),
        ],
        compiler_params=pltpu.CompilerParams(vmem_limit_bytes=16 * MB),
        name="grid",
    )(incoming)
    arrived = lax.all_to_all(filtered, "band", split_axis=0, concat_axis=0, tiled=True)
    combined = pl.pallas_call(
        direct_kernel,
        in_specs=specs("h", "h", "v", "v", "v", "v", "v"),
        out_specs=specs("v")[0],
        out_shape=jax.ShapeDtypeStruct((LEVELS * KPAD, 128), BF16),
        scratch_shapes=[
            pltpu.SMEM((BLOCKS,), jnp.int32),
            pltpu.SMEM((BLOCKS,), jnp.int32),
            pltpu.VMEM((8, 128, 128), BF16),
            pltpu.VMEM((3, 256, 128), F32),
            pltpu.VMEM((LEVELS * KPAD, 128), F32),
            pltpu.SemaphoreType.DMA((2,)),
        ],
        compiler_params=pltpu.CompilerParams(vmem_limit_bytes=16 * MB),
        name="direct",
    )(pos, base, arrived, lat_weights.reshape(1, LATS), drag, masked, legv)
    others = [
        lax.ppermute(combined, "lev", [(i, (i + s) % 4) for i in range(4)]) for s in (1, 2, 3)
    ]
    late_base, combined = lax.optimization_barrier((base, combined))
    gain, kron, coef = pl.pallas_call(
        prepare_kernel,
        in_specs=specs("s", "s", "s", "s", "v"),
        out_specs=specs("v", "v", "v"),
        out_shape=(
            pltpu.VMEM((ALL_LEVELS, KPAD, 128), F32),
            pltpu.VMEM((2, 128, 128), BF16),
            pltpu.VMEM((LEVELS * ALL_LEVELS, 128), F32),
        ),
        scratch_shapes=[pltpu.VMEM((KPAD, 128), F32)],
        compiler_params=pltpu.CompilerParams(vmem_limit_bytes=24 * MB),
        name="prepare",
    )(lev, late_base, level_modes, depths, mode_inverse)
    result = pl.pallas_call(
        vertical_kernel,
        in_specs=specs("v", "v", "v", "v", "v", "v", "v"),
        out_specs=specs("h")[0],
        out_shape=jax.ShapeDtypeStruct((BLOCKS * LEVELS, 128), F32),
        scratch_shapes=[
            pltpu.VMEM((BLOCKS * LEVELS, 128), F32),
            pltpu.SemaphoreType.DMA((KPAD // 8,)),
        ],
        compiler_params=pltpu.CompilerParams(vmem_limit_bytes=16 * MB),
        name="vertical",
    )(combined, *others, gain, kron, coef)
    return result.reshape(BLOCKS, LEVELS, 128)


def solution(mesh):
    placed = (
        P("band", "lev", None),
        P("band", None, None),
        P("band"),
        P("band"),
        P("band"),
        P(),
        P("lev", None, None),
        P(),
        P(),
        P(),
    )
    return jax.shard_map(
        on_device, mesh=mesh, in_specs=placed, out_specs=P("band", "lev", None), check_vma=False
    )
```

time: 82.2 us -> 68.4 us (0.83)
  local copies, waits for them, and re-layouts: 5.76 us -> 0.02 us
  waiting for transfers between devices: 6.89 us -> 1.67 us
  other arithmetic: 3.11 us -> 0 us
  blocking collectives: 45.5 us -> 43.4 us
  Pallas kernels: 16.9 us -> 18.2 us
  starting transfers between devices: 3.68 us -> 4.89 us
    unnamed x16 -> x10, local copies, waits for them, and re-layouts: 5.76 us -> 0.02 us
    ppermute x3, waiting for transfers between devices: 6.89 us -> 1.67 us  [on_device(): lax.ppermute(combined, 'lev', [(i, (i + s) % 4) for i in range(4)])]
    all_to_all x1, blocking collectives: 27.5 us -> 25.6 us  [on_device(): lax.all_to_all(outgoing.reshape(SOURCES, pairs, 2, 128), 'band', split_ax...]
    reduce_sum x3 -> x0, other arithmetic: 1.78 us -> none  [the longest x1 0.84 us: on_device(): jnp.sum(jnp.where(place[None, :] == slots[:4, None], wave_ids[None, :], 0...]
    pallas_call x3 -> x4, Pallas kernels: 13.6 us -> 15.2 us  [the longest x1 6.91 us: on_device(): pl.pallas_call(forward_kernel, in_specs=specs('h', 'h', 'h', 'h', 'h'), o...]
    ppermute x3, starting transfers between devices: 3.68 us -> 4.89 us  [on_device(): lax.ppermute(combined, 'lev', [(i, (i + s) % 4) for i in range(4)])]
  transfers between devices with their start and end apart: 3 -> 3, of which waited for: 3 -> 1; matrix products, arithmetic and copies ran while one was open for 0% -> 0% of each run, Pallas kernels for 0% -> 2%
where the time goes in v1:
time: 68.4 us; the launch traced here: 68.3 us
  blocking collectives  43.4 us (63%)
  Pallas kernels  18.2 us (27%)
  starting transfers between devices  4.89 us (7%)
  waiting for transfers between devices  1.67 us (2%)
    all_to_all x1, blocking collectives, on_device(): lax.all_to_all(outgoing.reshape(SOURCES, pairs, 2, 128), 'band', split_ax...  25.6 us
    all_to_all x1, blocking collectives, on_device(): lax.all_to_all(filtered, 'band', split_axis=0, concat_axis=0, tiled=True)  17.8 us
    pallas_call x1, Pallas kernels, on_device(): pl.pallas_call(forward_kernel, in_specs=specs('h', 'h', 'h', 'h', 'h'), o...  6.91 us
    pallas_call x1, Pallas kernels, on_device(): pl.pallas_call(direct_kernel, in_specs=specs('h', 'h', 'v', 'v', 'v', 'v'...  5.82 us
    ppermute x3, starting transfers between devices, on_device(): lax.ppermute(combined, 'lev', [(i, (i + s) % 4) for i in range(4)])  4.89 us
    pallas_call x1, Pallas kernels, on_device(): pl.pallas_call(grid_kernel, in_specs=specs('v'), out_specs=specs('v')[0],...  3.01 us
    ppermute x3, waiting for transfers between devices, on_device(): lax.ppermute(combined, 'lev', [(i, (i + s) % 4) for i in range(4)])  1.67 us
  transfers between devices with their start and end apart: 3, of which 1 were waited for; matrix products, arithmetic and copies ran while one was open for 0% of the time, Pallas kernels for 2%

profile of v1, /device:TPU:1, one launch (start us, length us, event | category | flops | bytes accessed | tf_op | source)
XLA Modules:
  0.0 68.3 jit_solution(17756957253979077712)
XLA Ops:
  0.0 0.0 copy-start.3
  0.0 0.0 copy-start
  0.0 0.0 copy-start.1
  0.0 0.0 copy-start.2
  0.0 0.0 copy-start.4
  0.0 6.9 %forward.1 = (bf16[1152,128]{1,0:T(8,128)(2,1)S(1)}, bf16[84,64,1024]{2,1,0:T(8,128)(2,1)S(1)}, f32[336,128]{1,0:T(8,128)S(1)}, s32[84]{0:T(128)S(1)}, s32[84]{0:T(128)S(1)}) custom-call(s32[8]{0:T(128)} %wave_hbm.1, s32[84]{0:T(128)} %slot_hbm.1, s32[84]{0:T(128)} %start_hbm.1, f32[336,128]{1,0:T(8,128)} %bitcast.9, bf16[84,64,1024]{2,1,0:T(8,128)(2,1)} %leg_hbm.1), custom_call_target="tpu_custom_call" | custom-call | tf_op jit(solution)/shard_map/forward/pallas_call | solution.py:380
  6.9 25.6 %all_to_all.10 = bf16[64,9,2,128]{3,2,1,0:T(2,128)(2,1)S(1)} all-to-all(bf16[64,9,2,128]{3,2,1,0:T(2,128)(2,1)S(1)} %bitcast.7), channel_id=1, replica_groups=mesh['band'=64,'lev'=4] {'band'}, dimensions={0} | all-to-all | bytes 589824 | tf_op jit(solution)/shard_map/all_to_all | solution.py:408
  32.5 3.0 %grid.1 = bf16[64,16,128]{2,1,0:T(8,128)(2,1)S(1)} custom-call(bf16[1152,128]{1,0:T(8,128)(2,1)S(1)} %bitcast.6), custom_call_target="tpu_custom_call" | custom-call | tf_op jit(solution)/shard_map/grid/pallas_call | solution.py:411
  35.6 17.8 %all_to_all.11.arrived_ref = bf16[64,16,128]{2,1,0:T(8,128)(2,1)S(1)} all-to-all(bf16[64,16,128]{2,1,0:T(8,128)(2,1)S(1)} %grid.1), channel_id=1, replica_groups=mesh['band'=64,'lev'=4] {'band'}, dimensions={0} | all-to-all | bytes 524288 | tf_op jit(solution)/shard_map/all_to_all | solution.py:425
  53.4 0.0 copy-done.3
  53.4 0.0 copy-done
  53.4 5.8 %direct.1.own_ref = bf16[352,128]{1,0:T(8,128)(2,1)S(1)} custom-call(s32[84]{0:T(128)S(1)} %get-tuple-element.16.pos_hbm, s32[84]{0:T(128)S(1)} %get-tuple-element.21.base_hbm.base_ref, bf16[64,16,128]{2,1,0:T(8,128)(2,1)S(1)} %all_to_all.11.arrived_ref, f32[1,1024]{1,0:T(1,128)S(1)} %bitcast.8, f32[4,2,1024]{2,1,0:T(2,128)S(1)} %copy-done, ...), custom_call_target="tpu_custom_call" | custom-call | tf_op jit(solution)/shard_map/direct/pallas_call | solution.py:426
  59.2 1.3 %collective-permute-start = (bf16[352,128]{1,0:T(8,128)(2,1)S(1)}, bf16[352,128]{1,0:T(8,128)(2,1)S(1)}, u32[]{:S(2)}, u32[]{:S(2)}) collective-permute-start(bf16[352,128]{1,0:T(8,128)(2,1)S(1)} %direct.1.own_ref), channel_id=1, source_target_pairs={{0,1},{1,2},{2,3},{3,0},{4,5},{5,6},{6,7},{7,4},{8,9},{9,10},{10,1... | collective-permute-start | bytes 270344 | tf_op jit(solution)/shard_map/ppermute | solution.py:443
  60.5 2.5 %collective-permute-start.1 = (bf16[352,128]{1,0:T(8,128)(2,1)S(1)}, bf16[352,128]{1,0:T(8,128)(2,1)S(1)}, u32[]{:S(2)}, u32[]{:S(2)}) collective-permute-start(bf16[352,128]{1,0:T(8,128)(2,1)S(1)} %direct.1.own_ref), channel_id=1, source_target_pairs={{0,2},{1,3},{2,0},{3,1},{4,6},{5,7},{6,4},{7,5},{8,10},{9,11},{10,... | collective-permute-start | bytes 270344 | tf_op jit(solution)/shard_map/ppermute | solution.py:443
  63.0 1.2 %collective-permute-start.2 = (bf16[352,128]{1,0:T(8,128)(2,1)S(1)}, bf16[352,128]{1,0:T(8,128)(2,1)S(1)}, u32[]{:S(2)}, u32[]{:S(2)}) collective-permute-start(bf16[352,128]{1,0:T(8,128)(2,1)S(1)} %direct.1.own_ref), channel_id=1, source_target_pairs={{0,3},{1,0},{2,1},{3,2},{4,7},{5,4},{6,5},{7,6},{8,11},{9,8},{10,9... | collective-permute-start | bytes 270344 | tf_op jit(solution)/shard_map/ppermute | solution.py:443
  64.1 0.0 copy-done.1
  64.1 0.0 copy-done.2
  64.1 0.0 copy-done.4
  64.1 1.3 %prepare.1 = (f32[16,88,128]{2,1,0:T(8,128)S(1)}, bf16[2,128,128]{2,1,0:T(8,128)(2,1)S(1)}, f32[64,128]{1,0:T(8,128)S(1)}) custom-call(s32[1]{0:T(128)} %bitcast.4.lev_ref, s32[84]{0:T(128)S(1)} %get-tuple-element.21.base_hbm.base_ref, f32[16,16]{1,0:T(8,128)S(1)} %copy-done.1, f32[16]{0:T(128)S(1)} %copy-done.4, f32[16,16]{1,0:T(8,128)S(1)} %copy-done.2), custom_call_target="tpu_custom_call" | custom-call | tf_op jit(solution)/shard_map/prepare/pallas_call | solution.py:446
  65.5 0.0 collective-permute-done.one_ref
  65.5 1.7 %collective-permute-done.1.two_ref = bf16[352,128]{1,0:T(8,128)(2,1)S(1)} collective-permute-done((bf16[352,128]{1,0:T(8,128)(2,1)S(1)}, bf16[352,128]{1,0:T(8,128)(2,1)S(1)}, u32[]{:S(2)}, u32[]{:S(2)}) %collective-permute-start.1) | collective-permute-done | bytes 90144 | tf_op jit(solution)/shard_map/ppermute | solution.py:443
  67.1 0.0 collective-permute-done.2.three_ref
  67.2 1.1 %vertical.1 = f32[336,128]{1,0:T(8,128)} custom-call(bf16[352,128]{1,0:T(8,128)(2,1)S(1)} %direct.1.own_ref, bf16[352,128]{1,0:T(8,128)(2,1)S(1)} %collective-permute-done.one_ref, bf16[352,128]{1,0:T(8,128)(2,1)S(1)} %collective-permute-done.1.two_ref, bf16[352,128]{1,0:T(8,128)(2,1)S(1)} %collective-permute-done.2.three_ref, ...), custom_call_target="tpu_custom_call" | custom-call | tf_op jit(solution)/shard_map/vertical/pallas_call | solution.py:459
Async XLA Ops:
  0.0 53.4 %copy-start.3 = (f32[1024]{0:T(1024)S(1)}, f32[1024]{0:T(1024)}, u32[]{:S(2)}) copy-start(f32[1024]{0:T(1024)} %param.15) | copy-start | bytes 12292
  0.0 53.4 %copy-start = (f32[4,2,1024]{2,1,0:T(2,128)S(1)}, f32[4,2,1024]{2,1,0:T(2,128)}, u32[]{:S(2)}) copy-start(f32[4,2,1024]{2,1,0:T(2,128)} %drag_ref.1) | copy-start | bytes 98308
  0.0 64.1 %copy-start.1 = (f32[16,16]{1,0:T(8,128)S(1)}, f32[16,16]{1,0:T(8,128)}, u32[]{:S(2)}) copy-start(f32[16,16]{1,0:T(8,128)} %level_ref.1) | copy-start | bytes 3076
  0.0 64.1 %copy-start.2 = (f32[16,16]{1,0:T(8,128)S(1)}, f32[16,16]{1,0:T(8,128)}, u32[]{:S(2)}) copy-start(f32[16,16]{1,0:T(8,128)} %mode_ref.1) | copy-start | bytes 3076
  0.0 64.1 %copy-start.4 = (f32[16]{0:T(128)S(1)}, f32[16]{0:T(128)}, u32[]{:S(2)}) copy-start(f32[16]{0:T(128)} %depth_ref.1) | copy-start | bytes 196
  59.2 6.2 %collective-permute-start = (bf16[352,128]{1,0:T(8,128)(2,1)S(1)}, bf16[352,128]{1,0:T(8,128)(2,1)S(1)}, u32[]{:S(2)}, u32[]{:S(2)}) collective-permute-start(bf16[352,128]{1,0:T(8,128)(2,1)S(1)} %direct.1.own_ref), channel_id=1, source_target_pairs={{0,1},{1,2},{2,3},{3,0},{4,5},{5,6},{6,7},{7,4},{8,9},{9,10},{10,1... | collective-permute-start | bytes 270344 | tf_op jit(solution)/shard_map/ppermute | solution.py:443
  60.5 6.6 %collective-permute-start.1 = (bf16[352,128]{1,0:T(8,128)(2,1)S(1)}, bf16[352,128]{1,0:T(8,128)(2,1)S(1)}, u32[]{:S(2)}, u32[]{:S(2)}) collective-permute-start(bf16[352,128]{1,0:T(8,128)(2,1)S(1)} %direct.1.own_ref), channel_id=1, source_target_pairs={{0,2},{1,3},{2,0},{3,1},{4,6},{5,7},{6,4},{7,5},{8,10},{9,11},{10,... | collective-permute-start | bytes 270344 | tf_op jit(solution)/shard_map/ppermute | solution.py:443
  63.0 4.2 %collective-permute-start.2 = (bf16[352,128]{1,0:T(8,128)(2,1)S(1)}, bf16[352,128]{1,0:T(8,128)(2,1)S(1)}, u32[]{:S(2)}, u32[]{:S(2)}) collective-permute-start(bf16[352,128]{1,0:T(8,128)(2,1)S(1)} %direct.1.own_ref), channel_id=1, source_target_pairs={{0,3},{1,0},{2,1},{3,2},{4,7},{5,4},{6,5},{7,6},{8,11},{9,8},{10,9... | collective-permute-start | bytes 270344 | tf_op jit(solution)/shard_map/ppermute | solution.py:443

commit v2 on v1

--- a/solution.py
+++ b/solution.py
@@ -20,6 +20,8 @@
 CHUNKS = BLOCKS // CHUNK
 KPAD = 88
 XPAD = 1152
+TURNED = 2
+AHEAD = 5
 XTILES = XPAD // 128
 F32 = jnp.float32
 BF16 = jnp.bfloat16
@@ -71,7 +73,7 @@
         )
         for c in range(CHUNKS)
     ]
-    for copy in copies:
+    for copy in copies[:AHEAD]:
         copy.start()
     for copy in inputs:
         copy.wait()
@@ -136,11 +138,18 @@
             lhs_ref[j, 32 * l + 16 : 32 * l + 32, :] = south.astype(BF16)
         return carry
 
-    lax.fori_loop(0, BLOCKS // 2, build, 0, unroll=6)
-
     half = CHUNK // 2
+
+    def build_chunk(c):
+        lax.fori_loop(c * half, (c + 1) * half, build, 0, unroll=half)
+
+    build_chunk(0)
     for c in range(CHUNKS):
         copies[c].wait()
+        if c + AHEAD < CHUNKS:
+            copies[c + AHEAD].start()
+        if c + 1 < CHUNKS:
+            build_chunk(c + 1)
         lhs = jnp.concatenate([lhs_ref[c * half + i] for i in range(half)], axis=1)
         for n in range(LATS // 256):
             rhs = legv_ref[c * CHUNK : (c + 1) * CHUNK, :, 256 * n : 256 * n + 256]
@@ -265,7 +274,7 @@
 
 def direct_kernel(
     pos_hbm, base_hbm, arrived_ref, weight_ref, drag_ref, masked_ref, legv_ref,
-    out_ref, pos_ref, base_ref, v_ref, acc_ref, comb_ref, small,
+    out_ref, pos_ref, base_ref, v_ref, acc_ref, comb_ref, turned_ref, small,
 ):
     inputs = [
         pltpu.make_async_copy(pos_hbm, pos_ref, small.at[0]),
@@ -312,18 +321,37 @@
             total = jnp.where(live, value[0:4] + masked_ref[pl.ds(4 * k, 4), :], 0.0)
             comb_ref[pl.ds(k, 4, stride=KPAD), :] = total
 
-    def groups_of(step, carry):
+    steps = BLOCKS // 12
+
+    def turn(step):
+        for part in range(TURNED):
+            group = 3 * step + part
+            for i in range(2):
+                for b in range(8):
+                    tile = legv_ref[
+                        4 * group + 2 * i : 4 * group + 2 * i + 2, :, 128 * b : 128 * b + 128
+                    ]
+                    turned_ref[2 * (step % 2) + part, i, 128 * b : 128 * b + 128, :] = (
+                        tile.reshape(128, 128).T
+                    )
+
+    turn(0)
+    for step in range(steps):
         lhs = jnp.concatenate([v_ref[b] for b in range(8)], axis=1)
-        for part in range(3):
+        if step + 1 < steps:
+            turn(step + 1)
+        for part in (2, 0, 1):
             group = 3 * step + part
-            rhs = legv_ref[pl.ds(4 * group, 4)].reshape(4 * ROWS, LATS)
-            product = lax.dot_general(
-                lhs, rhs, (((1,), (1,)), ((), ())), preferred_element_type=F32
-            )
-            finish(group, part, product)
-        return carry
-
-    lax.fori_loop(0, BLOCKS // 12, groups_of, 0)
+            if part < TURNED:
+                slot = 2 * (step % 2) + part
+                rhs = jnp.concatenate([turned_ref[slot, 0], turned_ref[slot, 1]], axis=1)
+                product = jnp.dot(lhs, rhs, preferred_element_type=F32)
+            else:
+                rhs = legv_ref[4 * group : 4 * group + 4].reshape(4 * ROWS, LATS)
+                product = lax.dot_general(
+                    lhs, rhs, (((1,), (1,)), ((), ())), preferred_element_type=F32
+                )
+            finish(group, part + 3 * (step % 2), product)
     out_ref[...] = comb_ref[...].astype(BF16)
 
 
@@ -432,8 +460,9 @@
             pltpu.SMEM((BLOCKS,), jnp.int32),
             pltpu.SMEM((BLOCKS,), jnp.int32),
             pltpu.VMEM((8, 128, 128), BF16),
-            pltpu.VMEM((3, 256, 128), F32),
+            pltpu.VMEM((6, 256, 128), F32),
             pltpu.VMEM((LEVELS * KPAD, 128), F32),
+            pltpu.VMEM((4, 2, LATS, 128), BF16),
             pltpu.SemaphoreType.DMA((2,)),
         ],
         compiler_params=pltpu.CompilerParams(vmem_limit_bytes=16 * MB),

time: 68.4 us -> 65.2 us (0.953)
  Pallas kernels: 18.2 us -> 15 us
    pallas_call x1, Pallas kernels: 5.82 us -> 3.72 us  [on_device(): pl.pallas_call(direct_kernel, in_specs=specs('h', 'h', 'v', 'v', 'v', 'v'...]
    pallas_call x1, Pallas kernels: 6.91 us -> 5.76 us  [on_device(): pl.pallas_call(forward_kernel, in_specs=specs('h', 'h', 'h', 'h', 'h'), o...]
where the time goes in v2:
time: 65.2 us; the launch traced here: 65 us
  blocking collectives  43.4 us (67%)
  Pallas kernels  15 us (23%)
  starting transfers between devices  4.89 us (7%)
  waiting for transfers between devices  1.69 us (3%)
    all_to_all x1, blocking collectives, on_device(): lax.all_to_all(outgoing.reshape(SOURCES, pairs, 2, 128), 'band', split_ax...  25.6 us
    all_to_all x1, blocking collectives, on_device(): lax.all_to_all(filtered, 'band', split_axis=0, concat_axis=0, tiled=True)  17.8 us
    pallas_call x1, Pallas kernels, on_device(): pl.pallas_call(forward_kernel, in_specs=specs('h', 'h', 'h', 'h', 'h'), o...  5.76 us
    ppermute x3, starting transfers between devices, on_device(): lax.ppermute(combined, 'lev', [(i, (i + s) % 4) for i in range(4)])  4.89 us
    pallas_call x1, Pallas kernels, on_device(): pl.pallas_call(direct_kernel, in_specs=specs('h', 'h', 'v', 'v', 'v', 'v'...  3.72 us
    pallas_call x1, Pallas kernels, on_device(): pl.pallas_call(grid_kernel, in_specs=specs('v'), out_specs=specs('v')[0],...  3.02 us
    ppermute x3, waiting for transfers between devices, on_device(): lax.ppermute(combined, 'lev', [(i, (i + s) % 4) for i in range(4)])  1.69 us
    pallas_call x1, Pallas kernels, on_device(): pl.pallas_call(prepare_kernel, in_specs=specs('s', 's', 's', 's', 'v'), o...  1.34 us
  transfers between devices with their start and end apart: 3, of which 1 were waited for; matrix products, arithmetic and copies ran while one was open for 0% of the time, Pallas kernels for 2%

profile of v2, /device:TPU:1, one launch (start us, length us, event | category | flops | bytes accessed | tf_op | source)
XLA Modules:
  0.0 65.0 jit_solution(16666330752100791488)
XLA Ops:
  0.0 0.0 copy-start.3
  0.0 0.0 copy-start
  0.0 0.0 copy-start.1
  0.0 0.0 copy-start.2
  0.0 0.0 copy-start.4
  0.0 5.8 %forward.1 = (bf16[1152,128]{1,0:T(8,128)(2,1)S(1)}, bf16[84,64,1024]{2,1,0:T(8,128)(2,1)S(1)}, f32[336,128]{1,0:T(8,128)S(1)}, s32[84]{0:T(128)S(1)}, s32[84]{0:T(128)S(1)}) custom-call(s32[8]{0:T(128)} %wave_hbm.1, s32[84]{0:T(128)} %slot_hbm.1, s32[84]{0:T(128)} %start_hbm.1, f32[336,128]{1,0:T(8,128)} %bitcast.9, bf16[84,64,1024]{2,1,0:T(8,128)(2,1)} %leg_hbm.1), custom_call_target="tpu_custom_call" | custom-call | tf_op jit(solution)/shard_map/forward/pallas_call | solution.py:408
  5.8 25.6 %all_to_all.10 = bf16[64,9,2,128]{3,2,1,0:T(2,128)(2,1)S(1)} all-to-all(bf16[64,9,2,128]{3,2,1,0:T(2,128)(2,1)S(1)} %bitcast.7), channel_id=1, replica_groups=mesh['band'=64,'lev'=4] {'band'}, dimensions={0} | all-to-all | bytes 589824 | tf_op jit(solution)/shard_map/all_to_all | solution.py:436
  31.4 3.0 %grid.1 = bf16[64,16,128]{2,1,0:T(8,128)(2,1)S(1)} custom-call(bf16[1152,128]{1,0:T(8,128)(2,1)S(1)} %bitcast.6), custom_call_target="tpu_custom_call" | custom-call | tf_op jit(solution)/shard_map/grid/pallas_call | solution.py:439
  34.4 17.8 %all_to_all.11.arrived_ref = bf16[64,16,128]{2,1,0:T(8,128)(2,1)S(1)} all-to-all(bf16[64,16,128]{2,1,0:T(8,128)(2,1)S(1)} %grid.1), channel_id=1, replica_groups=mesh['band'=64,'lev'=4] {'band'}, dimensions={0} | all-to-all | bytes 524288 | tf_op jit(solution)/shard_map/all_to_all | solution.py:453
  52.2 0.0 copy-done.3
  52.2 0.0 copy-done
  52.2 3.7 %direct.1.own_ref = bf16[352,128]{1,0:T(8,128)(2,1)S(1)} custom-call(s32[84]{0:T(128)S(1)} %get-tuple-element.16.pos_hbm, s32[84]{0:T(128)S(1)} %get-tuple-element.21.base_hbm.base_ref, bf16[64,16,128]{2,1,0:T(8,128)(2,1)S(1)} %all_to_all.11.arrived_ref, f32[1,1024]{1,0:T(1,128)S(1)} %bitcast.8, f32[4,2,1024]{2,1,0:T(2,128)S(1)} %copy-done, ...), custom_call_target="tpu_custom_call" | custom-call | tf_op jit(solution)/shard_map/direct/pallas_call | solution.py:454
  56.0 1.3 %collective-permute-start = (bf16[352,128]{1,0:T(8,128)(2,1)S(1)}, bf16[352,128]{1,0:T(8,128)(2,1)S(1)}, u32[]{:S(2)}, u32[]{:S(2)}) collective-permute-start(bf16[352,128]{1,0:T(8,128)(2,1)S(1)} %direct.1.own_ref), channel_id=1, source_target_pairs={{0,1},{1,2},{2,3},{3,0},{4,5},{5,6},{6,7},{7,4},{8,9},{9,10},{10,1... | collective-permute-start | bytes 270344 | tf_op jit(solution)/shard_map/ppermute | solution.py:472
  57.3 2.5 %collective-permute-start.1 = (bf16[352,128]{1,0:T(8,128)(2,1)S(1)}, bf16[352,128]{1,0:T(8,128)(2,1)S(1)}, u32[]{:S(2)}, u32[]{:S(2)}) collective-permute-start(bf16[352,128]{1,0:T(8,128)(2,1)S(1)} %direct.1.own_ref), channel_id=1, source_target_pairs={{0,2},{1,3},{2,0},{3,1},{4,6},{5,7},{6,4},{7,5},{8,10},{9,11},{10,... | collective-permute-start | bytes 270344 | tf_op jit(solution)/shard_map/ppermute | solution.py:472
  59.7 1.1 %collective-permute-start.2 = (bf16[352,128]{1,0:T(8,128)(2,1)S(1)}, bf16[352,128]{1,0:T(8,128)(2,1)S(1)}, u32[]{:S(2)}, u32[]{:S(2)}) collective-permute-start(bf16[352,128]{1,0:T(8,128)(2,1)S(1)} %direct.1.own_ref), channel_id=1, source_target_pairs={{0,3},{1,0},{2,1},{3,2},{4,7},{5,4},{6,5},{7,6},{8,11},{9,8},{10,9... | collective-permute-start | bytes 270344 | tf_op jit(solution)/shard_map/ppermute | solution.py:472
  60.8 0.0 copy-done.1
  60.9 0.0 copy-done.2
  60.9 0.0 copy-done.4
  60.9 1.3 %prepare.1 = (f32[16,88,128]{2,1,0:T(8,128)S(1)}, bf16[2,128,128]{2,1,0:T(8,128)(2,1)S(1)}, f32[64,128]{1,0:T(8,128)S(1)}) custom-call(s32[1]{0:T(128)} %bitcast.4.lev_ref, s32[84]{0:T(128)S(1)} %get-tuple-element.21.base_hbm.base_ref, f32[16,16]{1,0:T(8,128)S(1)} %copy-done.1, f32[16]{0:T(128)S(1)} %copy-done.4, f32[16,16]{1,0:T(8,128)S(1)} %copy-done.2), custom_call_target="tpu_custom_call" | custom-call | tf_op jit(solution)/shard_map/prepare/pallas_call | solution.py:475
  62.2 0.0 collective-permute-done.one_ref
  62.2 1.7 %collective-permute-done.1.two_ref = bf16[352,128]{1,0:T(8,128)(2,1)S(1)} collective-permute-done((bf16[352,128]{1,0:T(8,128)(2,1)S(1)}, bf16[352,128]{1,0:T(8,128)(2,1)S(1)}, u32[]{:S(2)}, u32[]{:S(2)}) %collective-permute-start.1) | collective-permute-done | bytes 90144 | tf_op jit(solution)/shard_map/ppermute | solution.py:472
  63.9 0.0 collective-permute-done.2.three_ref
  63.9 1.1 %vertical.1 = f32[336,128]{1,0:T(8,128)} custom-call(bf16[352,128]{1,0:T(8,128)(2,1)S(1)} %direct.1.own_ref, bf16[352,128]{1,0:T(8,128)(2,1)S(1)} %collective-permute-done.one_ref, bf16[352,128]{1,0:T(8,128)(2,1)S(1)} %collective-permute-done.1.two_ref, bf16[352,128]{1,0:T(8,128)(2,1)S(1)} %collective-permute-done.2.three_ref, ...), custom_call_target="tpu_custom_call" | custom-call | tf_op jit(solution)/shard_map/vertical/pallas_call | solution.py:488
Async XLA Ops:
  0.0 52.2 %copy-start.3 = (f32[1024]{0:T(1024)S(1)}, f32[1024]{0:T(1024)}, u32[]{:S(2)}) copy-start(f32[1024]{0:T(1024)} %param.15) | copy-start | bytes 12292
  0.0 52.2 %copy-start = (f32[4,2,1024]{2,1,0:T(2,128)S(1)}, f32[4,2,1024]{2,1,0:T(2,128)}, u32[]{:S(2)}) copy-start(f32[4,2,1024]{2,1,0:T(2,128)} %drag_ref.1) | copy-start | bytes 98308
  0.0 60.8 %copy-start.1 = (f32[16,16]{1,0:T(8,128)S(1)}, f32[16,16]{1,0:T(8,128)}, u32[]{:S(2)}) copy-start(f32[16,16]{1,0:T(8,128)} %level_ref.1) | copy-start | bytes 3076
  0.0 60.8 %copy-start.2 = (f32[16,16]{1,0:T(8,128)S(1)}, f32[16,16]{1,0:T(8,128)}, u32[]{:S(2)}) copy-start(f32[16,16]{1,0:T(8,128)} %mode_ref.1) | copy-start | bytes 3076
  0.0 60.8 %copy-start.4 = (f32[16]{0:T(128)S(1)}, f32[16]{0:T(128)}, u32[]{:S(2)}) copy-start(f32[16]{0:T(128)} %depth_ref.1) | copy-start | bytes 196
  56.0 6.2 %collective-permute-start = (bf16[352,128]{1,0:T(8,128)(2,1)S(1)}, bf16[352,128]{1,0:T(8,128)(2,1)S(1)}, u32[]{:S(2)}, u32[]{:S(2)}) collective-permute-start(bf16[352,128]{1,0:T(8,128)(2,1)S(1)} %direct.1.own_ref), channel_id=1, source_target_pairs={{0,1},{1,2},{2,3},{3,0},{4,5},{5,6},{6,7},{7,4},{8,9},{9,10},{10,1... | collective-permute-start | bytes 270344 | tf_op jit(solution)/shard_map/ppermute | solution.py:472
  57.3 6.6 %collective-permute-start.1 = (bf16[352,128]{1,0:T(8,128)(2,1)S(1)}, bf16[352,128]{1,0:T(8,128)(2,1)S(1)}, u32[]{:S(2)}, u32[]{:S(2)}) collective-permute-start(bf16[352,128]{1,0:T(8,128)(2,1)S(1)} %direct.1.own_ref), channel_id=1, source_target_pairs={{0,2},{1,3},{2,0},{3,1},{4,6},{5,7},{6,4},{7,5},{8,10},{9,11},{10,... | collective-permute-start | bytes 270344 | tf_op jit(solution)/shard_map/ppermute | solution.py:472
  59.7 4.2 %collective-permute-start.2 = (bf16[352,128]{1,0:T(8,128)(2,1)S(1)}, bf16[352,128]{1,0:T(8,128)(2,1)S(1)}, u32[]{:S(2)}, u32[]{:S(2)}) collective-permute-start(bf16[352,128]{1,0:T(8,128)(2,1)S(1)} %direct.1.own_ref), channel_id=1, source_target_pairs={{0,3},{1,0},{2,1},{3,2},{4,7},{5,4},{6,5},{7,6},{8,11},{9,8},{10,9... | collective-permute-start | bytes 270344 | tf_op jit(solution)/shard_map/ppermute | solution.py:472

commit v3 on v2

--- a/solution.py
+++ b/solution.py
@@ -73,8 +73,8 @@
         )
         for c in range(CHUNKS)
     ]
-    for copy in copies[:AHEAD]:
-        copy.start()
+    for c in range(AHEAD):
+        copies[c].start(priority=c % 2)
     for copy in inputs:
         copy.wait()
     lane = iota((8, 128), 1)
@@ -147,7 +147,7 @@
     for c in range(CHUNKS):
         copies[c].wait()
         if c + AHEAD < CHUNKS:
-            copies[c + AHEAD].start()
+            copies[c + AHEAD].start(priority=(c + AHEAD) % 2)
         if c + 1 < CHUNKS:
             build_chunk(c + 1)
         lhs = jnp.concatenate([lhs_ref[c * half + i] for i in range(half)], axis=1)

time: 65.2 us -> 64.3 us (0.986)
  Pallas kernels: 15 us -> 14.1 us
    pallas_call x1, Pallas kernels: 5.76 us -> 4.89 us  [on_device(): pl.pallas_call(forward_kernel, in_specs=specs('h', 'h', 'h', 'h', 'h'), o...]
where the time goes in v3:
time: 64.3 us; the launch traced here: 64.1 us
  blocking collectives  43.4 us (67%)
  Pallas kernels  14.1 us (22%)
  starting transfers between devices  4.9 us (8%)
  waiting for transfers between devices  1.66 us (3%)
    all_to_all x1, blocking collectives, on_device(): lax.all_to_all(outgoing.reshape(SOURCES, pairs, 2, 128), 'band', split_ax...  25.6 us
    all_to_all x1, blocking collectives, on_device(): lax.all_to_all(filtered, 'band', split_axis=0, concat_axis=0, tiled=True)  17.8 us
    ppermute x3, starting transfers between devices, on_device(): lax.ppermute(combined, 'lev', [(i, (i + s) % 4) for i in range(4)])  4.9 us
    pallas_call x1, Pallas kernels, on_device(): pl.pallas_call(forward_kernel, in_specs=specs('h', 'h', 'h', 'h', 'h'), o...  4.89 us
    pallas_call x1, Pallas kernels, on_device(): pl.pallas_call(direct_kernel, in_specs=specs('h', 'h', 'v', 'v', 'v', 'v'...  3.71 us
    pallas_call x1, Pallas kernels, on_device(): pl.pallas_call(grid_kernel, in_specs=specs('v'), out_specs=specs('v')[0],...  3.02 us
    ppermute x3, waiting for transfers between devices, on_device(): lax.ppermute(combined, 'lev', [(i, (i + s) % 4) for i in range(4)])  1.66 us
    pallas_call x1, Pallas kernels, on_device(): pl.pallas_call(prepare_kernel, in_specs=specs('s', 's', 's', 's', 'v'), o...  1.34 us
  transfers between devices with their start and end apart: 3, of which 1 were waited for; matrix products, arithmetic and copies ran while one was open for 0% of the time, Pallas kernels for 2%

profile of v3, /device:TPU:1, one launch (start us, length us, event | category | flops | bytes accessed | tf_op | source)
XLA Modules:
  0.0 64.1 jit_solution(14071910730022119099)
XLA Ops:
  0.0 0.0 copy-start.3
  0.0 0.0 copy-start
  0.0 0.0 copy-start.1
  0.0 0.0 copy-start.2
  0.0 0.0 copy-start.4
  0.0 4.9 %forward.1 = (bf16[1152,128]{1,0:T(8,128)(2,1)S(1)}, bf16[84,64,1024]{2,1,0:T(8,128)(2,1)S(1)}, f32[336,128]{1,0:T(8,128)S(1)}, s32[84]{0:T(128)S(1)}, s32[84]{0:T(128)S(1)}) custom-call(s32[8]{0:T(128)} %wave_hbm.1, s32[84]{0:T(128)} %slot_hbm.1, s32[84]{0:T(128)} %start_hbm.1, f32[336,128]{1,0:T(8,128)} %bitcast.9, bf16[84,64,1024]{2,1,0:T(8,128)(2,1)} %leg_hbm.1), custom_call_target="tpu_custom_call" | custom-call | tf_op jit(solution)/shard_map/forward/pallas_call | solution.py:408
  4.9 25.6 %all_to_all.10 = bf16[64,9,2,128]{3,2,1,0:T(2,128)(2,1)S(1)} all-to-all(bf16[64,9,2,128]{3,2,1,0:T(2,128)(2,1)S(1)} %bitcast.7), channel_id=1, replica_groups=mesh['band'=64,'lev'=4] {'band'}, dimensions={0} | all-to-all | bytes 589824 | tf_op jit(solution)/shard_map/all_to_all | solution.py:436
  30.5 3.0 %grid.1 = bf16[64,16,128]{2,1,0:T(8,128)(2,1)S(1)} custom-call(bf16[1152,128]{1,0:T(8,128)(2,1)S(1)} %bitcast.6), custom_call_target="tpu_custom_call" | custom-call | tf_op jit(solution)/shard_map/grid/pallas_call | solution.py:439
  33.5 17.8 %all_to_all.11.arrived_ref = bf16[64,16,128]{2,1,0:T(8,128)(2,1)S(1)} all-to-all(bf16[64,16,128]{2,1,0:T(8,128)(2,1)S(1)} %grid.1), channel_id=1, replica_groups=mesh['band'=64,'lev'=4] {'band'}, dimensions={0} | all-to-all | bytes 524288 | tf_op jit(solution)/shard_map/all_to_all | solution.py:453
  51.4 0.0 copy-done.3
  51.4 0.0 copy-done
  51.4 3.7 %direct.1.own_ref = bf16[352,128]{1,0:T(8,128)(2,1)S(1)} custom-call(s32[84]{0:T(128)S(1)} %get-tuple-element.16.pos_hbm, s32[84]{0:T(128)S(1)} %get-tuple-element.21.base_hbm.base_ref, bf16[64,16,128]{2,1,0:T(8,128)(2,1)S(1)} %all_to_all.11.arrived_ref, f32[1,1024]{1,0:T(1,128)S(1)} %bitcast.8, f32[4,2,1024]{2,1,0:T(2,128)S(1)} %copy-done, ...), custom_call_target="tpu_custom_call" | custom-call | tf_op jit(solution)/shard_map/direct/pallas_call | solution.py:454
  55.1 1.3 %collective-permute-start = (bf16[352,128]{1,0:T(8,128)(2,1)S(1)}, bf16[352,128]{1,0:T(8,128)(2,1)S(1)}, u32[]{:S(2)}, u32[]{:S(2)}) collective-permute-start(bf16[352,128]{1,0:T(8,128)(2,1)S(1)} %direct.1.own_ref), channel_id=1, source_target_pairs={{0,1},{1,2},{2,3},{3,0},{4,5},{5,6},{6,7},{7,4},{8,9},{9,10},{10,1... | collective-permute-start | bytes 270344 | tf_op jit(solution)/shard_map/ppermute | solution.py:472
  56.4 2.4 %collective-permute-start.1 = (bf16[352,128]{1,0:T(8,128)(2,1)S(1)}, bf16[352,128]{1,0:T(8,128)(2,1)S(1)}, u32[]{:S(2)}, u32[]{:S(2)}) collective-permute-start(bf16[352,128]{1,0:T(8,128)(2,1)S(1)} %direct.1.own_ref), channel_id=1, source_target_pairs={{0,2},{1,3},{2,0},{3,1},{4,6},{5,7},{6,4},{7,5},{8,10},{9,11},{10,... | collective-permute-start | bytes 270344 | tf_op jit(solution)/shard_map/ppermute | solution.py:472
  58.8 1.2 %collective-permute-start.2 = (bf16[352,128]{1,0:T(8,128)(2,1)S(1)}, bf16[352,128]{1,0:T(8,128)(2,1)S(1)}, u32[]{:S(2)}, u32[]{:S(2)}) collective-permute-start(bf16[352,128]{1,0:T(8,128)(2,1)S(1)} %direct.1.own_ref), channel_id=1, source_target_pairs={{0,3},{1,0},{2,1},{3,2},{4,7},{5,4},{6,5},{7,6},{8,11},{9,8},{10,9... | collective-permute-start | bytes 270344 | tf_op jit(solution)/shard_map/ppermute | solution.py:472
  60.0 0.0 copy-done.1
  60.0 0.0 copy-done.2
  60.0 0.0 copy-done.4
  60.0 1.3 %prepare.1 = (f32[16,88,128]{2,1,0:T(8,128)S(1)}, bf16[2,128,128]{2,1,0:T(8,128)(2,1)S(1)}, f32[64,128]{1,0:T(8,128)S(1)}) custom-call(s32[1]{0:T(128)} %bitcast.4.lev_ref, s32[84]{0:T(128)S(1)} %get-tuple-element.21.base_hbm.base_ref, f32[16,16]{1,0:T(8,128)S(1)} %copy-done.1, f32[16]{0:T(128)S(1)} %copy-done.4, f32[16,16]{1,0:T(8,128)S(1)} %copy-done.2), custom_call_target="tpu_custom_call" | custom-call | tf_op jit(solution)/shard_map/prepare/pallas_call | solution.py:475
  61.3 0.0 collective-permute-done.one_ref
  61.4 1.7 %collective-permute-done.1.two_ref = bf16[352,128]{1,0:T(8,128)(2,1)S(1)} collective-permute-done((bf16[352,128]{1,0:T(8,128)(2,1)S(1)}, bf16[352,128]{1,0:T(8,128)(2,1)S(1)}, u32[]{:S(2)}, u32[]{:S(2)}) %collective-permute-start.1) | collective-permute-done | bytes 90144 | tf_op jit(solution)/shard_map/ppermute | solution.py:472
  63.0 0.0 collective-permute-done.2.three_ref
  63.0 1.1 %vertical.1 = f32[336,128]{1,0:T(8,128)} custom-call(bf16[352,128]{1,0:T(8,128)(2,1)S(1)} %direct.1.own_ref, bf16[352,128]{1,0:T(8,128)(2,1)S(1)} %collective-permute-done.one_ref, bf16[352,128]{1,0:T(8,128)(2,1)S(1)} %collective-permute-done.1.two_ref, bf16[352,128]{1,0:T(8,128)(2,1)S(1)} %collective-permute-done.2.three_ref, ...), custom_call_target="tpu_custom_call" | custom-call | tf_op jit(solution)/shard_map/vertical/pallas_call | solution.py:488
Async XLA Ops:
  0.0 51.4 %copy-start.3 = (f32[1024]{0:T(1024)S(1)}, f32[1024]{0:T(1024)}, u32[]{:S(2)}) copy-start(f32[1024]{0:T(1024)} %param.15) | copy-start | bytes 12292
  0.0 51.4 %copy-start = (f32[4,2,1024]{2,1,0:T(2,128)S(1)}, f32[4,2,1024]{2,1,0:T(2,128)}, u32[]{:S(2)}) copy-start(f32[4,2,1024]{2,1,0:T(2,128)} %drag_ref.1) | copy-start | bytes 98308
  0.0 60.0 %copy-start.1 = (f32[16,16]{1,0:T(8,128)S(1)}, f32[16,16]{1,0:T(8,128)}, u32[]{:S(2)}) copy-start(f32[16,16]{1,0:T(8,128)} %level_ref.1) | copy-start | bytes 3076
  0.0 60.0 %copy-start.2 = (f32[16,16]{1,0:T(8,128)S(1)}, f32[16,16]{1,0:T(8,128)}, u32[]{:S(2)}) copy-start(f32[16,16]{1,0:T(8,128)} %mode_ref.1) | copy-start | bytes 3076
  0.0 60.0 %copy-start.4 = (f32[16]{0:T(128)S(1)}, f32[16]{0:T(128)}, u32[]{:S(2)}) copy-start(f32[16]{0:T(128)} %depth_ref.1) | copy-start | bytes 196
  55.1 6.3 %collective-permute-start = (bf16[352,128]{1,0:T(8,128)(2,1)S(1)}, bf16[352,128]{1,0:T(8,128)(2,1)S(1)}, u32[]{:S(2)}, u32[]{:S(2)}) collective-permute-start(bf16[352,128]{1,0:T(8,128)(2,1)S(1)} %direct.1.own_ref), channel_id=1, source_target_pairs={{0,1},{1,2},{2,3},{3,0},{4,5},{5,6},{6,7},{7,4},{8,9},{9,10},{10,1... | collective-permute-start | bytes 270344 | tf_op jit(solution)/shard_map/ppermute | solution.py:472
  56.4 6.6 %collective-permute-start.1 = (bf16[352,128]{1,0:T(8,128)(2,1)S(1)}, bf16[352,128]{1,0:T(8,128)(2,1)S(1)}, u32[]{:S(2)}, u32[]{:S(2)}) collective-permute-start(bf16[352,128]{1,0:T(8,128)(2,1)S(1)} %direct.1.own_ref), channel_id=1, source_target_pairs={{0,2},{1,3},{2,0},{3,1},{4,6},{5,7},{6,4},{7,5},{8,10},{9,11},{10,... | collective-permute-start | bytes 270344 | tf_op jit(solution)/shard_map/ppermute | solution.py:472
  58.8 4.2 %collective-permute-start.2 = (bf16[352,128]{1,0:T(8,128)(2,1)S(1)}, bf16[352,128]{1,0:T(8,128)(2,1)S(1)}, u32[]{:S(2)}, u32[]{:S(2)}) collective-permute-start(bf16[352,128]{1,0:T(8,128)(2,1)S(1)} %direct.1.own_ref), channel_id=1, source_target_pairs={{0,3},{1,0},{2,1},{3,2},{4,7},{5,4},{6,5},{7,6},{8,11},{9,8},{10,9... | collective-permute-start | bytes 270344 | tf_op jit(solution)/shard_map/ppermute | solution.py:472

commit v4 on v3

--- a/solution.py
+++ b/solution.py
@@ -20,7 +20,7 @@
 CHUNKS = BLOCKS // CHUNK
 KPAD = 88
 XPAD = 1152
-TURNED = 2
+TURNED = (2, 1, 2, 1, 2, 2, 1)
 AHEAD = 5
 XTILES = XPAD // 128
 F32 = jnp.float32
@@ -226,9 +226,10 @@
                 c1 = jnp.concatenate([shift[a][0]] * 4, axis=0)
                 s1 = jnp.concatenate([shift[a][1]] * 4, axis=0)
                 tw_ref[0, a, rows, :] = cos.astype(BF16)
-                tw_ref[1, a, rows, :] = sin.astype(BF16)
-                tw_ref[2, a, rows, :] = (c1 * cos + s1 * sin).astype(BF16)
                 tw_ref[3, a, rows, :] = (s1 * cos - c1 * sin).astype(BF16)
+                if a + 1 < XTILES:
+                    tw_ref[1, a, rows, :] = sin.astype(BF16)
+                    tw_ref[2, a, rows, :] = (c1 * cos + s1 * sin).astype(BF16)
                 if a + 1 < XTILES:
                     cos, sin = cos * step_cos - sin * step_sin, sin * step_cos + cos * step_sin
 
@@ -237,7 +238,7 @@
         jnp.concatenate([rows_of(f + p) for p in range(4)], axis=0).T.astype(BF16)
         for f in first_row
     ]
-    for a in range(XTILES):
+    for a in range(XTILES - 1):
         ce, se, co, so = [
             jnp.dot(spectra[i], tw_ref[i, a], preferred_element_type=F32) for i in range(4)
         ]
@@ -249,23 +250,32 @@
         ]
         s12, d12, s34, d34 = f1 + f2, f1 - f2, f3 + f4, f3 - f4
         folded = (s12 + s34, s12 - s34, d12 + d34, d12 - d34)
-        if a == 0:
-            share = jnp.where(iota((1, 128), 1) == 0, 0.5, 1.0)
-        else:
-            share = jnp.where(iota((1, 128), 1) == 0, 0.5, 0.0)
         for i in range(4):
             value = folded[i]
-            if a in (0, XTILES - 1):
-                value = value * share
+            if a == 0:
+                value = value * jnp.where(iota((1, 128), 1) == 0, 0.5, 1.0)
             g_ref[i, a] = value.astype(BF16)
+    last = XTILES - 1
+    ce, so = [jnp.dot(spectra[i], tw_ref[i, last], preferred_element_type=F32) for i in (0, 3)]
+    f1, f2 = [v * jnp.abs(v) for v in (ce - so, ce + so)]
+    only = jnp.where(iota((1, 128), 1) == 0, 1.0, 0.0)
+    g_ref[0, last] = ((f1 + f2) * only).astype(BF16)
+    g_ref[3, last] = ((f1 - f2) * only).astype(BF16)
     scale = 1.0 / (512.0 * 64.0)
     for i in range(4):
         total = lax.dot_general(
-            jnp.concatenate([tw_ref[i, a] for a in range(XTILES)], axis=1),
-            jnp.concatenate([g_ref[i, a] for a in range(XTILES)], axis=1),
+            jnp.concatenate([tw_ref[i, a] for a in range(last)], axis=1),
+            jnp.concatenate([g_ref[i, a] for a in range(last)], axis=1),
             (((1,), (1,)), ((), ())),
             preferred_element_type=F32,
         )
+        if i in (0, 3):
+            total = total + lax.dot_general(
+                tw_ref[i, last],
+                g_ref[i, last],
+                (((1,), (1,)), ((), ())),
+                preferred_element_type=F32,
+            )
         total = total * (scale if i % 2 == 0 else -scale)
         for p in range(4):
             send_ref[pl.ds(first_row[i] + p, SOURCES, stride=16), :] = total[64 * p : 64 * p + 64]
@@ -282,6 +292,21 @@
     ]
     for copy in inputs:
         copy.start()
+    steps = BLOCKS // 12
+
+    def turn(step):
+        for part in range(TURNED[step]):
+            group = 3 * step + part
+            for i in range(2):
+                for b in range(8):
+                    tile = legv_ref[
+                        4 * group + 2 * i : 4 * group + 2 * i + 2, :, 128 * b : 128 * b + 128
+                    ]
+                    turned_ref[2 * (step % 2) + part, i, 128 * b : 128 * b + 128, :] = (
+                        tile.reshape(128, 128).T
+                    )
+
+    turn(0)
     for b in range(8):
         cols = slice(128 * b, 128 * b + 128)
         weight = -weight_ref[0:1, cols]
@@ -321,28 +346,13 @@
             total = jnp.where(live, value[0:4] + masked_ref[pl.ds(4 * k, 4), :], 0.0)
             comb_ref[pl.ds(k, 4, stride=KPAD), :] = total
 
-    steps = BLOCKS // 12
-
-    def turn(step):
-        for part in range(TURNED):
-            group = 3 * step + part
-            for i in range(2):
-                for b in range(8):
-                    tile = legv_ref[
-                        4 * group + 2 * i : 4 * group + 2 * i + 2, :, 128 * b : 128 * b + 128
-                    ]
-                    turned_ref[2 * (step % 2) + part, i, 128 * b : 128 * b + 128, :] = (
-                        tile.reshape(128, 128).T
-                    )
-
-    turn(0)
     for step in range(steps):
         lhs = jnp.concatenate([v_ref[b] for b in range(8)], axis=1)
         if step + 1 < steps:
             turn(step + 1)
         for part in (2, 0, 1):
             group = 3 * step + part
-            if part < TURNED:
+            if part < TURNED[step]:
                 slot = 2 * (step % 2) + part
                 rhs = jnp.concatenate([turned_ref[slot, 0], turned_ref[slot, 1]], axis=1)
                 product = jnp.dot(lhs, rhs, preferred_element_type=F32)

time: 64.3 us -> 63.9 us (level)
  no operation moved by 1% of the time
where the time goes in v4:
time: 63.9 us; the launch traced here: 63.8 us
  blocking collectives  43.4 us (68%)
  Pallas kernels  13.7 us (21%)
  starting transfers between devices  4.9 us (8%)
  waiting for transfers between devices  1.67 us (3%)
    all_to_all x1, blocking collectives, on_device(): lax.all_to_all(outgoing.reshape(SOURCES, pairs, 2, 128), 'band', split_ax...  25.6 us
    all_to_all x1, blocking collectives, on_device(): lax.all_to_all(filtered, 'band', split_axis=0, concat_axis=0, tiled=True)  17.8 us
    ppermute x3, starting transfers between devices, on_device(): lax.ppermute(combined, 'lev', [(i, (i + s) % 4) for i in range(4)])  4.9 us
    pallas_call x1, Pallas kernels, on_device(): pl.pallas_call(forward_kernel, in_specs=specs('h', 'h', 'h', 'h', 'h'), o...  4.89 us
    pallas_call x1, Pallas kernels, on_device(): pl.pallas_call(direct_kernel, in_specs=specs('h', 'h', 'v', 'v', 'v', 'v'...  3.54 us
    pallas_call x1, Pallas kernels, on_device(): pl.pallas_call(grid_kernel, in_specs=specs('v'), out_specs=specs('v')[0],...  2.85 us
    ppermute x3, waiting for transfers between devices, on_device(): lax.ppermute(combined, 'lev', [(i, (i + s) % 4) for i in range(4)])  1.67 us
    pallas_call x1, Pallas kernels, on_device(): pl.pallas_call(prepare_kernel, in_specs=specs('s', 's', 's', 's', 'v'), o...  1.34 us
  transfers between devices with their start and end apart: 3, of which 1 were waited for; matrix products, arithmetic and copies ran while one was open for 0% of the time, Pallas kernels for 2%

profile of v4, /device:TPU:1, one launch (start us, length us, event | category | flops | bytes accessed | tf_op | source)
XLA Modules:
  0.0 63.8 jit_solution(3750426734609270637)
XLA Ops:
  0.0 0.0 copy-start.3
  0.0 0.0 copy-start
  0.0 0.0 copy-start.1
  0.0 0.0 copy-start.2
  0.0 0.0 copy-start.4
  0.0 4.9 %forward.1 = (bf16[1152,128]{1,0:T(8,128)(2,1)S(1)}, bf16[84,64,1024]{2,1,0:T(8,128)(2,1)S(1)}, f32[336,128]{1,0:T(8,128)S(1)}, s32[84]{0:T(128)S(1)}, s32[84]{0:T(128)S(1)}) custom-call(s32[8]{0:T(128)} %wave_hbm.1, s32[84]{0:T(128)} %slot_hbm.1, s32[84]{0:T(128)} %start_hbm.1, f32[336,128]{1,0:T(8,128)} %bitcast.9, bf16[84,64,1024]{2,1,0:T(8,128)(2,1)} %leg_hbm.1), custom_call_target="tpu_custom_call" | custom-call | tf_op jit(solution)/shard_map/forward/pallas_call | solution.py:418
  4.9 25.6 %all_to_all.10 = bf16[64,9,2,128]{3,2,1,0:T(2,128)(2,1)S(1)} all-to-all(bf16[64,9,2,128]{3,2,1,0:T(2,128)(2,1)S(1)} %bitcast.7), channel_id=1, replica_groups=mesh['band'=64,'lev'=4] {'band'}, dimensions={0} | all-to-all | bytes 589824 | tf_op jit(solution)/shard_map/all_to_all | solution.py:446
  30.5 2.8 %grid.1 = bf16[64,16,128]{2,1,0:T(8,128)(2,1)S(1)} custom-call(bf16[1152,128]{1,0:T(8,128)(2,1)S(1)} %bitcast.6), custom_call_target="tpu_custom_call" | custom-call | tf_op jit(solution)/shard_map/grid/pallas_call | solution.py:449
  33.4 17.8 %all_to_all.11.arrived_ref = bf16[64,16,128]{2,1,0:T(8,128)(2,1)S(1)} all-to-all(bf16[64,16,128]{2,1,0:T(8,128)(2,1)S(1)} %grid.1), channel_id=1, replica_groups=mesh['band'=64,'lev'=4] {'band'}, dimensions={0} | all-to-all | bytes 524288 | tf_op jit(solution)/shard_map/all_to_all | solution.py:463
  51.2 0.0 copy-done.3
  51.2 0.0 copy-done
  51.2 3.5 %direct.1.own_ref = bf16[352,128]{1,0:T(8,128)(2,1)S(1)} custom-call(s32[84]{0:T(128)S(1)} %get-tuple-element.16.pos_hbm, s32[84]{0:T(128)S(1)} %get-tuple-element.21.base_hbm.base_ref, bf16[64,16,128]{2,1,0:T(8,128)(2,1)S(1)} %all_to_all.11.arrived_ref, f32[1,1024]{1,0:T(1,128)S(1)} %bitcast.8, f32[4,2,1024]{2,1,0:T(2,128)S(1)} %copy-done, ...), custom_call_target="tpu_custom_call" | custom-call | tf_op jit(solution)/shard_map/direct/pallas_call | solution.py:464
  54.7 1.3 %collective-permute-start = (bf16[352,128]{1,0:T(8,128)(2,1)S(1)}, bf16[352,128]{1,0:T(8,128)(2,1)S(1)}, u32[]{:S(2)}, u32[]{:S(2)}) collective-permute-start(bf16[352,128]{1,0:T(8,128)(2,1)S(1)} %direct.1.own_ref), channel_id=1, source_target_pairs={{0,1},{1,2},{2,3},{3,0},{4,5},{5,6},{6,7},{7,4},{8,9},{9,10},{10,1... | collective-permute-start | bytes 270344 | tf_op jit(solution)/shard_map/ppermute | solution.py:482
  56.0 2.4 %collective-permute-start.1 = (bf16[352,128]{1,0:T(8,128)(2,1)S(1)}, bf16[352,128]{1,0:T(8,128)(2,1)S(1)}, u32[]{:S(2)}, u32[]{:S(2)}) collective-permute-start(bf16[352,128]{1,0:T(8,128)(2,1)S(1)} %direct.1.own_ref), channel_id=1, source_target_pairs={{0,2},{1,3},{2,0},{3,1},{4,6},{5,7},{6,4},{7,5},{8,10},{9,11},{10,... | collective-permute-start | bytes 270344 | tf_op jit(solution)/shard_map/ppermute | solution.py:482
  58.5 1.2 %collective-permute-start.2 = (bf16[352,128]{1,0:T(8,128)(2,1)S(1)}, bf16[352,128]{1,0:T(8,128)(2,1)S(1)}, u32[]{:S(2)}, u32[]{:S(2)}) collective-permute-start(bf16[352,128]{1,0:T(8,128)(2,1)S(1)} %direct.1.own_ref), channel_id=1, source_target_pairs={{0,3},{1,0},{2,1},{3,2},{4,7},{5,4},{6,5},{7,6},{8,11},{9,8},{10,9... | collective-permute-start | bytes 270344 | tf_op jit(solution)/shard_map/ppermute | solution.py:482
  59.6 0.0 copy-done.1
  59.6 0.0 copy-done.2
  59.6 0.0 copy-done.4
  59.7 1.3 %prepare.1 = (f32[16,88,128]{2,1,0:T(8,128)S(1)}, bf16[2,128,128]{2,1,0:T(8,128)(2,1)S(1)}, f32[64,128]{1,0:T(8,128)S(1)}) custom-call(s32[1]{0:T(128)} %bitcast.4.lev_ref, s32[84]{0:T(128)S(1)} %get-tuple-element.21.base_hbm.base_ref, f32[16,16]{1,0:T(8,128)S(1)} %copy-done.1, f32[16]{0:T(128)S(1)} %copy-done.4, f32[16,16]{1,0:T(8,128)S(1)} %copy-done.2), custom_call_target="tpu_custom_call" | custom-call | tf_op jit(solution)/shard_map/prepare/pallas_call | solution.py:485
  61.0 0.0 collective-permute-done.one_ref
  61.0 1.7 %collective-permute-done.1.two_ref = bf16[352,128]{1,0:T(8,128)(2,1)S(1)} collective-permute-done((bf16[352,128]{1,0:T(8,128)(2,1)S(1)}, bf16[352,128]{1,0:T(8,128)(2,1)S(1)}, u32[]{:S(2)}, u32[]{:S(2)}) %collective-permute-start.1) | collective-permute-done | bytes 90144 | tf_op jit(solution)/shard_map/ppermute | solution.py:482
  62.7 0.0 collective-permute-done.2.three_ref
  62.7 1.1 %vertical.1 = f32[336,128]{1,0:T(8,128)} custom-call(bf16[352,128]{1,0:T(8,128)(2,1)S(1)} %direct.1.own_ref, bf16[352,128]{1,0:T(8,128)(2,1)S(1)} %collective-permute-done.one_ref, bf16[352,128]{1,0:T(8,128)(2,1)S(1)} %collective-permute-done.1.two_ref, bf16[352,128]{1,0:T(8,128)(2,1)S(1)} %collective-permute-done.2.three_ref, ...), custom_call_target="tpu_custom_call" | custom-call | tf_op jit(solution)/shard_map/vertical/pallas_call | solution.py:498
Async XLA Ops:
  0.0 51.2 %copy-start.3 = (f32[1024]{0:T(1024)S(1)}, f32[1024]{0:T(1024)}, u32[]{:S(2)}) copy-start(f32[1024]{0:T(1024)} %param.15) | copy-start | bytes 12292
  0.0 51.2 %copy-start = (f32[4,2,1024]{2,1,0:T(2,128)S(1)}, f32[4,2,1024]{2,1,0:T(2,128)}, u32[]{:S(2)}) copy-start(f32[4,2,1024]{2,1,0:T(2,128)} %drag_ref.1) | copy-start | bytes 98308
  0.0 59.6 %copy-start.1 = (f32[16,16]{1,0:T(8,128)S(1)}, f32[16,16]{1,0:T(8,128)}, u32[]{:S(2)}) copy-start(f32[16,16]{1,0:T(8,128)} %level_ref.1) | copy-start | bytes 3076
  0.0 59.6 %copy-start.2 = (f32[16,16]{1,0:T(8,128)S(1)}, f32[16,16]{1,0:T(8,128)}, u32[]{:S(2)}) copy-start(f32[16,16]{1,0:T(8,128)} %mode_ref.1) | copy-start | bytes 3076
  0.0 59.6 %copy-start.4 = (f32[16]{0:T(128)S(1)}, f32[16]{0:T(128)}, u32[]{:S(2)}) copy-start(f32[16]{0:T(128)} %depth_ref.1) | copy-start | bytes 196
  54.7 6.3 %collective-permute-start = (bf16[352,128]{1,0:T(8,128)(2,1)S(1)}, bf16[352,128]{1,0:T(8,128)(2,1)S(1)}, u32[]{:S(2)}, u32[]{:S(2)}) collective-permute-start(bf16[352,128]{1,0:T(8,128)(2,1)S(1)} %direct.1.own_ref), channel_id=1, source_target_pairs={{0,1},{1,2},{2,3},{3,0},{4,5},{5,6},{6,7},{7,4},{8,9},{9,10},{10,1... | collective-permute-start | bytes 270344 | tf_op jit(solution)/shard_map/ppermute | solution.py:482
  56.0 6.6 %collective-permute-start.1 = (bf16[352,128]{1,0:T(8,128)(2,1)S(1)}, bf16[352,128]{1,0:T(8,128)(2,1)S(1)}, u32[]{:S(2)}, u32[]{:S(2)}) collective-permute-start(bf16[352,128]{1,0:T(8,128)(2,1)S(1)} %direct.1.own_ref), channel_id=1, source_target_pairs={{0,2},{1,3},{2,0},{3,1},{4,6},{5,7},{6,4},{7,5},{8,10},{9,11},{10,... | collective-permute-start | bytes 270344 | tf_op jit(solution)/shard_map/ppermute | solution.py:482
  58.5 4.2 %collective-permute-start.2 = (bf16[352,128]{1,0:T(8,128)(2,1)S(1)}, bf16[352,128]{1,0:T(8,128)(2,1)S(1)}, u32[]{:S(2)}, u32[]{:S(2)}) collective-permute-start(bf16[352,128]{1,0:T(8,128)(2,1)S(1)} %direct.1.own_ref), channel_id=1, source_target_pairs={{0,3},{1,0},{2,1},{3,2},{4,7},{5,4},{6,5},{7,6},{8,11},{9,8},{10,9... | collective-permute-start | bytes 270344 | tf_op jit(solution)/shard_map/ppermute | solution.py:482

commit v5 on v4

--- a/solution.py
+++ b/solution.py
@@ -22,6 +22,7 @@
 XPAD = 1152
 TURNED = (2, 1, 2, 1, 2, 2, 1)
 AHEAD = 5
+OUT_TILES = (3, 6, 8, 10)
 XTILES = XPAD // 128
 F32 = jnp.float32
 BF16 = jnp.bfloat16
@@ -393,9 +394,15 @@
         count = min(8, BLOCKS - 8 * t)
         for l in range(LEVELS):
             out_ref[pl.ds(32 * t + l, count, stride=LEVELS), :] = results[l][0:count]
-        rows = pl.ds(32 * t, 4 * count)
-        copies.append(pltpu.make_async_copy(out_ref.at[rows], out_hbm.at[rows], sems.at[t]))
-        copies[-1].start()
+        if t in OUT_TILES:
+            first = 32 * (0 if not copies else OUT_TILES[len(copies) - 1] + 1)
+            rows = pl.ds(first, 32 * t + 4 * count - first)
+            copies.append(
+                pltpu.make_async_copy(
+                    out_ref.at[rows], out_hbm.at[rows], sems.at[len(copies)]
+                )
+            )
+            copies[-1].start(priority=len(copies) % 2)
     for copy in copies:
         copy.wait()
 
@@ -502,7 +509,7 @@
         out_shape=jax.ShapeDtypeStruct((BLOCKS * LEVELS, 128), F32),
         scratch_shapes=[
             pltpu.VMEM((BLOCKS * LEVELS, 128), F32),
-            pltpu.SemaphoreType.DMA((KPAD // 8,)),
+            pltpu.SemaphoreType.DMA((len(OUT_TILES),)),
         ],
         compiler_params=pltpu.CompilerParams(vmem_limit_bytes=16 * MB),
         name="vertical",

time: 63.9 us -> 63.9 us (level)
  no operation moved by 1% of the time
where the time goes in v5:
time: 63.9 us; the launch traced here: 63.7 us
  blocking collectives  43.4 us (68%)
  Pallas kernels  13.7 us (21%)
  starting transfers between devices  4.9 us (8%)
  waiting for transfers between devices  1.66 us (3%)
    all_to_all x1, blocking collectives, on_device(): lax.all_to_all(outgoing.reshape(SOURCES, pairs, 2, 128), 'band', split_ax...  25.6 us
    all_to_all x1, blocking collectives, on_device(): lax.all_to_all(filtered, 'band', split_axis=0, concat_axis=0, tiled=True)  17.8 us
    ppermute x3, starting transfers between devices, on_device(): lax.ppermute(combined, 'lev', [(i, (i + s) % 4) for i in range(4)])  4.9 us
    pallas_call x1, Pallas kernels, on_device(): pl.pallas_call(forward_kernel, in_specs=specs('h', 'h', 'h', 'h', 'h'), o...  4.89 us
    pallas_call x1, Pallas kernels, on_device(): pl.pallas_call(direct_kernel, in_specs=specs('h', 'h', 'v', 'v', 'v', 'v'...  3.54 us
    pallas_call x1, Pallas kernels, on_device(): pl.pallas_call(grid_kernel, in_specs=specs('v'), out_specs=specs('v')[0],...  2.85 us
    ppermute x3, waiting for transfers between devices, on_device(): lax.ppermute(combined, 'lev', [(i, (i + s) % 4) for i in range(4)])  1.66 us
    pallas_call x1, Pallas kernels, on_device(): pl.pallas_call(prepare_kernel, in_specs=specs('s', 's', 's', 's', 'v'), o...  1.34 us
  transfers between devices with their start and end apart: 3, of which 1 were waited for; matrix products, arithmetic and copies ran while one was open for 0% of the time, Pallas kernels for 2%

profile of v5, /device:TPU:1, one launch (start us, length us, event | category | flops | bytes accessed | tf_op | source)
XLA Modules:
  0.0 63.7 jit_solution(17724386909921443592)
XLA Ops:
  0.0 0.0 copy-start.3
  0.0 0.0 copy-start
  0.0 0.0 copy-start.1
  0.0 0.0 copy-start.2
  0.0 0.0 copy-start.4
  0.0 4.9 %forward.1 = (bf16[1152,128]{1,0:T(8,128)(2,1)S(1)}, bf16[84,64,1024]{2,1,0:T(8,128)(2,1)S(1)}, f32[336,128]{1,0:T(8,128)S(1)}, s32[84]{0:T(128)S(1)}, s32[84]{0:T(128)S(1)}) custom-call(s32[8]{0:T(128)} %wave_hbm.1, s32[84]{0:T(128)} %slot_hbm.1, s32[84]{0:T(128)} %start_hbm.1, f32[336,128]{1,0:T(8,128)} %bitcast.9, bf16[84,64,1024]{2,1,0:T(8,128)(2,1)} %leg_hbm.1), custom_call_target="tpu_custom_call" | custom-call | tf_op jit(solution)/shard_map/forward/pallas_call | solution.py:425
  4.9 25.6 %all_to_all.10 = bf16[64,9,2,128]{3,2,1,0:T(2,128)(2,1)S(1)} all-to-all(bf16[64,9,2,128]{3,2,1,0:T(2,128)(2,1)S(1)} %bitcast.7), channel_id=1, replica_groups=mesh['band'=64,'lev'=4] {'band'}, dimensions={0} | all-to-all | bytes 589824 | tf_op jit(solution)/shard_map/all_to_all | solution.py:453
  30.5 2.8 %grid.1 = bf16[64,16,128]{2,1,0:T(8,128)(2,1)S(1)} custom-call(bf16[1152,128]{1,0:T(8,128)(2,1)S(1)} %bitcast.6), custom_call_target="tpu_custom_call" | custom-call | tf_op jit(solution)/shard_map/grid/pallas_call | solution.py:456
  33.4 17.8 %all_to_all.11.arrived_ref = bf16[64,16,128]{2,1,0:T(8,128)(2,1)S(1)} all-to-all(bf16[64,16,128]{2,1,0:T(8,128)(2,1)S(1)} %grid.1), channel_id=1, replica_groups=mesh['band'=64,'lev'=4] {'band'}, dimensions={0} | all-to-all | bytes 524288 | tf_op jit(solution)/shard_map/all_to_all | solution.py:470
  51.2 0.0 copy-done.3
  51.2 0.0 copy-done
  51.2 3.5 %direct.1.own_ref = bf16[352,128]{1,0:T(8,128)(2,1)S(1)} custom-call(s32[84]{0:T(128)S(1)} %get-tuple-element.16.pos_hbm, s32[84]{0:T(128)S(1)} %get-tuple-element.21.base_hbm.base_ref, bf16[64,16,128]{2,1,0:T(8,128)(2,1)S(1)} %all_to_all.11.arrived_ref, f32[1,1024]{1,0:T(1,128)S(1)} %bitcast.8, f32[4,2,1024]{2,1,0:T(2,128)S(1)} %copy-done, ...), custom_call_target="tpu_custom_call" | custom-call | tf_op jit(solution)/shard_map/direct/pallas_call | solution.py:471
  54.7 1.3 %collective-permute-start = (bf16[352,128]{1,0:T(8,128)(2,1)S(1)}, bf16[352,128]{1,0:T(8,128)(2,1)S(1)}, u32[]{:S(2)}, u32[]{:S(2)}) collective-permute-start(bf16[352,128]{1,0:T(8,128)(2,1)S(1)} %direct.1.own_ref), channel_id=1, source_target_pairs={{0,1},{1,2},{2,3},{3,0},{4,5},{5,6},{6,7},{7,4},{8,9},{9,10},{10,1... | collective-permute-start | bytes 270344 | tf_op jit(solution)/shard_map/ppermute | solution.py:489
  56.0 2.4 %collective-permute-start.1 = (bf16[352,128]{1,0:T(8,128)(2,1)S(1)}, bf16[352,128]{1,0:T(8,128)(2,1)S(1)}, u32[]{:S(2)}, u32[]{:S(2)}) collective-permute-start(bf16[352,128]{1,0:T(8,128)(2,1)S(1)} %direct.1.own_ref), channel_id=1, source_target_pairs={{0,2},{1,3},{2,0},{3,1},{4,6},{5,7},{6,4},{7,5},{8,10},{9,11},{10,... | collective-permute-start | bytes 270344 | tf_op jit(solution)/shard_map/ppermute | solution.py:489
  58.5 1.2 %collective-permute-start.2 = (bf16[352,128]{1,0:T(8,128)(2,1)S(1)}, bf16[352,128]{1,0:T(8,128)(2,1)S(1)}, u32[]{:S(2)}, u32[]{:S(2)}) collective-permute-start(bf16[352,128]{1,0:T(8,128)(2,1)S(1)} %direct.1.own_ref), channel_id=1, source_target_pairs={{0,3},{1,0},{2,1},{3,2},{4,7},{5,4},{6,5},{7,6},{8,11},{9,8},{10,9... | collective-permute-start | bytes 270344 | tf_op jit(solution)/shard_map/ppermute | solution.py:489
  59.6 0.0 copy-done.1
  59.6 0.0 copy-done.2
  59.6 0.0 copy-done.4
  59.7 1.3 %prepare.1 = (f32[16,88,128]{2,1,0:T(8,128)S(1)}, bf16[2,128,128]{2,1,0:T(8,128)(2,1)S(1)}, f32[64,128]{1,0:T(8,128)S(1)}) custom-call(s32[1]{0:T(128)} %bitcast.4.lev_ref, s32[84]{0:T(128)S(1)} %get-tuple-element.21.base_hbm.base_ref, f32[16,16]{1,0:T(8,128)S(1)} %copy-done.1, f32[16]{0:T(128)S(1)} %copy-done.4, f32[16,16]{1,0:T(8,128)S(1)} %copy-done.2), custom_call_target="tpu_custom_call" | custom-call | tf_op jit(solution)/shard_map/prepare/pallas_call | solution.py:492
  61.0 0.0 collective-permute-done.one_ref
  61.0 1.7 %collective-permute-done.1.two_ref = bf16[352,128]{1,0:T(8,128)(2,1)S(1)} collective-permute-done((bf16[352,128]{1,0:T(8,128)(2,1)S(1)}, bf16[352,128]{1,0:T(8,128)(2,1)S(1)}, u32[]{:S(2)}, u32[]{:S(2)}) %collective-permute-start.1) | collective-permute-done | bytes 90144 | tf_op jit(solution)/shard_map/ppermute | solution.py:489
  62.7 0.0 collective-permute-done.2.three_ref
  62.7 1.1 %vertical.1 = f32[336,128]{1,0:T(8,128)} custom-call(bf16[352,128]{1,0:T(8,128)(2,1)S(1)} %direct.1.own_ref, bf16[352,128]{1,0:T(8,128)(2,1)S(1)} %collective-permute-done.one_ref, bf16[352,128]{1,0:T(8,128)(2,1)S(1)} %collective-permute-done.1.two_ref, bf16[352,128]{1,0:T(8,128)(2,1)S(1)} %collective-permute-done.2.three_ref, ...), custom_call_target="tpu_custom_call" | custom-call | tf_op jit(solution)/shard_map/vertical/pallas_call | solution.py:505
Async XLA Ops:
  0.0 51.2 %copy-start.3 = (f32[1024]{0:T(1024)S(1)}, f32[1024]{0:T(1024)}, u32[]{:S(2)}) copy-start(f32[1024]{0:T(1024)} %param.15) | copy-start | bytes 12292
  0.0 51.2 %copy-start = (f32[4,2,1024]{2,1,0:T(2,128)S(1)}, f32[4,2,1024]{2,1,0:T(2,128)}, u32[]{:S(2)}) copy-start(f32[4,2,1024]{2,1,0:T(2,128)} %drag_ref.1) | copy-start | bytes 98308
  0.0 59.6 %copy-start.1 = (f32[16,16]{1,0:T(8,128)S(1)}, f32[16,16]{1,0:T(8,128)}, u32[]{:S(2)}) copy-start(f32[16,16]{1,0:T(8,128)} %level_ref.1) | copy-start | bytes 3076
  0.0 59.6 %copy-start.2 = (f32[16,16]{1,0:T(8,128)S(1)}, f32[16,16]{1,0:T(8,128)}, u32[]{:S(2)}) copy-start(f32[16,16]{1,0:T(8,128)} %mode_ref.1) | copy-start | bytes 3076
  0.0 59.6 %copy-start.4 = (f32[16]{0:T(128)S(1)}, f32[16]{0:T(128)}, u32[]{:S(2)}) copy-start(f32[16]{0:T(128)} %depth_ref.1) | copy-start | bytes 196
  54.7 6.3 %collective-permute-start = (bf16[352,128]{1,0:T(8,128)(2,1)S(1)}, bf16[352,128]{1,0:T(8,128)(2,1)S(1)}, u32[]{:S(2)}, u32[]{:S(2)}) collective-permute-start(bf16[352,128]{1,0:T(8,128)(2,1)S(1)} %direct.1.own_ref), channel_id=1, source_target_pairs={{0,1},{1,2},{2,3},{3,0},{4,5},{5,6},{6,7},{7,4},{8,9},{9,10},{10,1... | collective-permute-start | bytes 270344 | tf_op jit(solution)/shard_map/ppermute | solution.py:489
  56.0 6.6 %collective-permute-start.1 = (bf16[352,128]{1,0:T(8,128)(2,1)S(1)}, bf16[352,128]{1,0:T(8,128)(2,1)S(1)}, u32[]{:S(2)}, u32[]{:S(2)}) collective-permute-start(bf16[352,128]{1,0:T(8,128)(2,1)S(1)} %direct.1.own_ref), channel_id=1, source_target_pairs={{0,2},{1,3},{2,0},{3,1},{4,6},{5,7},{6,4},{7,5},{8,10},{9,11},{10,... | collective-permute-start | bytes 270344 | tf_op jit(solution)/shard_map/ppermute | solution.py:489
  58.5 4.2 %collective-permute-start.2 = (bf16[352,128]{1,0:T(8,128)(2,1)S(1)}, bf16[352,128]{1,0:T(8,128)(2,1)S(1)}, u32[]{:S(2)}, u32[]{:S(2)}) collective-permute-start(bf16[352,128]{1,0:T(8,128)(2,1)S(1)} %direct.1.own_ref), channel_id=1, source_target_pairs={{0,3},{1,0},{2,1},{3,2},{4,7},{5,4},{6,5},{7,6},{8,11},{9,8},{10,9... | collective-permute-start | bytes 270344 | tf_op jit(solution)/shard_map/ppermute | solution.py:489
